TPU v7x, 128 devices: a whole 4x4x4 slice. The times are simulated.
128 devices in a mesh: grp: 8 (over x, y_hi), shard: 16 (over z, y_lo, core).
Axes of the slice: x: 4, y: 4 (y_hi: 2, y_lo: 2; y = y_hi * 2 + y_lo), z: 4, core: 2. Of those that a mesh axis runs over, the one named last changes fastest.
Arguments:
- points: bfloat16 [8, 24576, 1024], P('grp', 'shard'), may hold values from -6 to 6
- centroids: bfloat16 [8, 1024, 1024], P('grp', 'shard'), may hold values from -1.5 to 1.5
- tile_counts: int32 [8], replicated, may hold values from 97 to 192, as said below
Outputs:
- new_centroids: float32 [8, 1024, 1024], P('grp', 'shard')
- posterior_rows: bfloat16 [8, 24576, 1024], P('grp', 'shard')
Inputs may be any that keep to these rules, and one draw needn't show every extreme that they name: `tile_counts`: every coarse cluster has more than half of its 192 tile slots live, and some cluster has all 192.
All inputs are finite; a program needn't handle non-finite values.
Results may differ from a plain program's by a relative error of at most 0.0076.
Values may be sent and summed in bfloat16 or wider, within the bound.
A program may use at most 64 MiB of HBM per device.

v0:
```python
import jax
import jax.numpy as jnp
from jax import lax
from jax.sharding import PartitionSpec as P

TILE = 128
ITERS = 2


sharpness_factor = 48.0
epsilon = 1e-06


def partner(value, axis, bit):
    mask = 2**bit
    pairs = [(source, source ^ mask) for source in range(lax.axis_size(axis))]
    return lax.ppermute(value, axis, pairs)


def rms_unit(values):
    return values * lax.rsqrt(jnp.mean(values * values, axis=-1, keepdims=True) + epsilon)


def pick_entry(lookup_table, wanted):
    positions = jnp.arange(lookup_table.shape[0], dtype=jnp.int32)
    return jnp.sum(jnp.where(positions == wanted, lookup_table, 0))


def held_tiles(tile_total, shard_place, shard_count, slot_count):
    return jnp.clip((tile_total - shard_place + shard_count - 1) // shard_count, 0, slot_count)


def tile_weights(rows_per_tile, centroid_table):
    affinity_scores = lax.dot_general(
        rows_per_tile, centroid_table, (((1,), (1,)), ((), ())), preferred_element_type=jnp.float32
    ) * (sharpness_factor / rows_per_tile.shape[-1])
    exponent_terms = jnp.exp(affinity_scores)
    return (exponent_terms / jnp.sum(exponent_terms, axis=-1, keepdims=True)).astype(jnp.bfloat16)


def sweep(tile_stack, tile_limit, centroid_table, with_rows):
    centroid_count = centroid_table.shape[0]
    zero_sums = jnp.zeros((centroid_count, tile_stack.shape[2]), jnp.float32)
    zero_rows = jnp.zeros(tile_stack.shape, jnp.bfloat16)

    def visit(position, state_pair):
        running_sums, mean_rows = state_pair
        rows_per_tile = lax.dynamic_index_in_dim(tile_stack, position, 0, keepdims=False)
        weights = tile_weights(rows_per_tile, centroid_table)
        running_sums = running_sums + lax.dot_general(
            weights, rows_per_tile, (((0,), (0,)), ((), ())), preferred_element_type=jnp.float32
        )
        if with_rows:
            blended = jnp.dot(weights, centroid_table, preferred_element_type=jnp.float32).astype(
                jnp.bfloat16
            )
            mean_rows = lax.dynamic_update_index_in_dim(mean_rows, blended, position, 0)
        return (running_sums, mean_rows)

    return lax.fori_loop(0, tile_limit, visit, (zero_sums, zero_rows))


def body(points, centroids, tile_counts):
    slot_count = points.shape[1] // TILE
    half_slots = slot_count // 2
    feature_width = points.shape[2]
    shard_count = lax.axis_size("shard")
    shard_place = lax.axis_index("shard")
    group_index = lax.axis_index("grp")
    levels = lax.axis_size("grp").bit_length() - 1
    partner_bit = levels - 1
    unit_embeddings = rms_unit(points[0].astype(jnp.float32)).astype(jnp.bfloat16)
    tile_stack = unit_embeddings.reshape(slot_count, TILE, feature_width)
    own_held = held_tiles(
        pick_entry(tile_counts, group_index), shard_place, shard_count, slot_count
    )
    partner_group = jnp.bitwise_xor(group_index, 1 << partner_bit)
    partner_held = held_tiles(
        pick_entry(tile_counts, partner_group), shard_place, shard_count, slot_count
    )
    current_shard = centroids[0]
    borrowed = partner(tile_stack[half_slots:], "grp", partner_bit)
    updated = None
    out_rows = None
    for iteration in range(ITERS):
        is_last = iteration == ITERS - 1
        centroid_table = lax.all_gather(current_shard, "shard", axis=0, tiled=True)
        lent_piece = partner(current_shard, "grp", partner_bit)
        lent_table = lax.all_gather(lent_piece, "shard", axis=0, tiled=True)
        own_total, rows_low = sweep(
            tile_stack[:half_slots], jnp.minimum(own_held, half_slots), centroid_table, is_last
        )
        lent_limit = jnp.clip(partner_held - half_slots, 0, slot_count - half_slots)
        lent_total, rows_high = sweep(borrowed, lent_limit, lent_table, is_last)
        own_reduced, lent_reduced = (
            lax.psum_scatter(own_total, "shard", scatter_dimension=0, tiled=True),
            lax.psum_scatter(lent_total, "shard", scatter_dimension=0, tiled=True),
        )
        own_reduced = own_reduced + partner(lent_reduced, "grp", partner_bit)
        if is_last:
            returned_rows = partner(rows_high, "grp", partner_bit)
            out_rows = jnp.concatenate([rows_low, returned_rows], axis=0)
        updated = rms_unit(own_reduced)
        current_shard = updated.astype(jnp.bfloat16)
    return (updated[None], out_rows.reshape(1, slot_count * TILE, feature_width))


def solution(mesh):
    return jax.shard_map(
        body,
        mesh=mesh,
        in_specs=(P("grp", "shard", None), P("grp", "shard", None), P()),
        out_specs=(P("grp", "shard", None), P("grp", "shard", None)),
        check_vma=False,
    )
```

profile of v0, /device:TPU:0, one launch (start us, length us, event | category | flops | bytes accessed | tf_op | source)
XLA Modules:
  0.0 488.7 jit_solution(12478442984499041312)
XLA Ops:
  24.2 32.1 %collective-permute-done = bf16[6,128,1024]{2,1,0:T(8,128)(2,1)S(1)} collective-permute-done((bf16[6,128,1024]{2,1,0:T(8,128)(2,1)S(1)}, bf16[6,128,1024]{2,1,0:T(8,128)(2,1)S(1)}, u32[]{:S(2)}, u32[]{:S(2)}) %collective-permute-start) | collective-permute-done | bytes 1572896 | tf_op jit(solution)/shard_map/ppermute | solution.py:17
  59.9 20.9 %while.45 = (s32[]{:T(128)}, f32[1024,1024]{1,0:T(8,128)}, s32[]{:T(128)}, bf16[6,128,1024]{2,1,0:T(8,128)(2,1)}, bf16[1024,1024]{1,0:T(8,128)(2,1)S(1)}, /*index=5*/s32[]{:T(128)}, s32[]{:T(128)}, s32[]{:T(128)}) while((s32[]{:T(128)}, f32[1024,1024]{1,0:T(8,128)}, s32[]{:T(128)}, bf16[6,128,1024]{2,1,0:T(8,128)(2,1)}, ...), condition=%wide.region_9.10_spmd, body=%wide.region_7.9_spmd.sunk | while | flops 538443648 | bytes 12059783 | solution.py:60
  68.7 5.1 %convolution_add_fusion.9 = f32[1024,1024]{1,0:T(8,128)} fusion(f32[1024,1024]{1,0:T(8,128)} %get-tuple-element.381, f32[128,1024]{1,0:T(8,128)S(1)} %get-tuple-element.330, f32[128]{0:T(128)S(1)} %get-tuple-element.331, bf16[6,128,1024]{2,1,0:T(8,128)(2,1)} %get-tuple-element.391, s32[]{:T(128)S(6)} %select_n.46), kind=kOutput, calls=%fused_computation.11.clone.1 | convolution fusion | flops 269746176 | bytes 9175556 | tf_op jit(solution)/shard_map/while/body/dot_general | solution.py:50
  75.7 5.1 %convolution_add_fusion.9 = f32[1024,1024]{1,0:T(8,128)} fusion(f32[1024,1024]{1,0:T(8,128)} %get-tuple-element.381, f32[128,1024]{1,0:T(8,128)S(1)} %get-tuple-element.330, f32[128]{0:T(128)S(1)} %get-tuple-element.331, bf16[6,128,1024]{2,1,0:T(8,128)(2,1)} %get-tuple-element.391, s32[]{:T(128)S(6)} %select_n.46), kind=kOutput, calls=%fused_computation.11.clone.1 | convolution fusion | flops 269746176 | bytes 9175556 | tf_op jit(solution)/shard_map/while/body/dot_general | solution.py:50
  81.6 5.4 %all-gather.12.cloned.1.call-done = bf16[1,1024,1024]{2,1,0:T(8,128)(2,1)} async-done(((bf16[1,64,1024]{2,1,0:T(8,128)(2,1)}), bf16[1,1024,1024]{2,1,0:T(8,128)(2,1)}) %all-gather.12.cloned.1.call-update) | async-done | bytes 2097168 | tf_op jit(solution)/shard_map/all_gather | solution.py:87
  89.5 41.7 %while.44 = (s32[]{:T(128)}, f32[1024,1024]{1,0:T(8,128)}, s32[]{:T(128)}, bf16[6,128,1024]{2,1,0:T(8,128)(2,1)}, bf16[1024,1024]{1,0:T(8,128)(2,1)S(1)}, /*index=5*/s32[]{:T(128)}, s32[]{:T(128)}, s32[]{:T(128)}) while((s32[]{:T(128)}, f32[1024,1024]{1,0:T(8,128)}, s32[]{:T(128)}, bf16[6,128,1024]{2,1,0:T(8,128)(2,1)}, ...), condition=%wide.region_4.5_spmd, body=%wide.region_2.4_spmd.sunk | while | flops 538443648 | bytes 12059783 | solution.py:60
  98.3 5.1 %convolution_add_fusion.8 = f32[1024,1024]{1,0:T(8,128)} fusion(f32[1024,1024]{1,0:T(8,128)} %get-tuple-element.357, f32[128,1024]{1,0:T(8,128)S(1)} %get-tuple-element.323, f32[128]{0:T(128)S(1)} %get-tuple-element.324, bf16[6,128,1024]{2,1,0:T(8,128)(2,1)} %get-tuple-element.367, s32[]{:T(128)S(6)} %select_n.45), kind=kOutput, calls=%fused_computation.clone.1 | convolution fusion | flops 269746176 | bytes 9175556 | tf_op jit(solution)/shard_map/while/body/dot_general | solution.py:50
  119.1 5.1 %convolution_add_fusion.8 = f32[1024,1024]{1,0:T(8,128)} fusion(f32[1024,1024]{1,0:T(8,128)} %get-tuple-element.357, f32[128,1024]{1,0:T(8,128)S(1)} %get-tuple-element.323, f32[128]{0:T(128)S(1)} %get-tuple-element.324, bf16[6,128,1024]{2,1,0:T(8,128)(2,1)} %get-tuple-element.367, s32[]{:T(128)S(6)} %select_n.45), kind=kOutput, calls=%fused_computation.clone.1 | convolution fusion | flops 269746176 | bytes 9175556 | tf_op jit(solution)/shard_map/while/body/dot_general | solution.py:50
  126.1 5.1 %convolution_add_fusion.8 = f32[1024,1024]{1,0:T(8,128)} fusion(f32[1024,1024]{1,0:T(8,128)} %get-tuple-element.357, f32[128,1024]{1,0:T(8,128)S(1)} %get-tuple-element.323, f32[128]{0:T(128)S(1)} %get-tuple-element.324, bf16[6,128,1024]{2,1,0:T(8,128)(2,1)} %get-tuple-element.367, s32[]{:T(128)S(6)} %select_n.45), kind=kOutput, calls=%fused_computation.clone.1 | convolution fusion | flops 269746176 | bytes 9175556 | tf_op jit(solution)/shard_map/while/body/dot_general | solution.py:50
  131.3 41.3 %reduce-scatter.7.cloned.1.call-done = f32[64,1024]{1,0:T(8,128)} async-done(((f32[1024,1024]{1,0:T(8,128)}), f32[64,1024]{1,0:T(8,128)}) %reduce-scatter.7.cloned.1.call-update) | async-done | bytes 262160 | tf_op jit(solution)/shard_map/reduce_scatter | solution.py:97
  175.5 69.1 %reduce-scatter.5.cloned.1.call-done = f32[64,1024]{1,0:T(8,128)} async-done(((f32[1024,1024]{1,0:T(8,128)}), f32[64,1024]{1,0:T(8,128)}) %reduce-scatter.5.cloned.1.call-update) | async-done | bytes 262160 | tf_op jit(solution)/shard_map/reduce_scatter | solution.py:96
  253.7 32.1 %all-gather.10.cloned.1.call-done = bf16[1024,1024]{1,0:T(8,128)(2,1)} async-done(((bf16[64,1024]{1,0:T(8,128)(2,1)}), bf16[1024,1024]{1,0:T(8,128)(2,1)}) %all-gather.10.cloned.1.call-update) | async-done | bytes 2097168 | tf_op jit(solution)/shard_map/all_gather | solution.py:89
  289.7 24.5 %while.47 = (s32[]{:T(128)}, f32[1024,1024]{1,0:T(8,128)}, bf16[6,128,1024]{2,1,0:T(8,128)(2,1)}, s32[]{:T(128)}, bf16[6,128,1024]{2,1,0:T(8,128)(2,1)}, /*index...) while((s32[]{:T(128)}, f32[1024,1024]{1,0:T(8,128)}, bf16[6,128,1024]{2,1,0:T(8,128)(2,1)}, ...), condition=%wide.region_18.19_spmd, body=%wide.region_16.18_spmd.sunk | while | flops 807272320 | bytes 14943891 | solution.py:60
  299.7 5.1 %convolution_add_fusion.11 = f32[1024,1024]{1,0:T(8,128)} fusion(f32[1024,1024]{1,0:T(8,128)} %get-tuple-element.433, bf16[6,128,1024]{2,1,0:T(8,128)(2,1)} %get-tuple-element.445, s32[]{:T(128)S(6)} %select_n.48, f32[128,1024]{1,0:T(8,128)S(1)} %get-tuple-element.346, f32[128]{0:T(128)S(1)} %get-tuple-element.347), kind=kOutput, calls=%fused_computation.35.clone.1 | convolution fusion | flops 269746176 | bytes 9175556 | tf_op jit(solution)/shard_map/while/body/dot_general | solution.py:50
  307.9 5.1 %convolution_add_fusion.11 = f32[1024,1024]{1,0:T(8,128)} fusion(f32[1024,1024]{1,0:T(8,128)} %get-tuple-element.433, bf16[6,128,1024]{2,1,0:T(8,128)(2,1)} %get-tuple-element.445, s32[]{:T(128)S(6)} %select_n.48, f32[128,1024]{1,0:T(8,128)S(1)} %get-tuple-element.346, f32[128]{0:T(128)S(1)} %get-tuple-element.347), kind=kOutput, calls=%fused_computation.35.clone.1 | convolution fusion | flops 269746176 | bytes 9175556 | tf_op jit(solution)/shard_map/while/body/dot_general | solution.py:50
  314.3 7.5 %all-gather.8.cloned.1.call-done = bf16[1024,1024]{1,0:T(8,128)(2,1)} async-done(((bf16[64,1024]{1,0:T(8,128)(2,1)}), bf16[1024,1024]{1,0:T(8,128)(2,1)}) %all-gather.8.cloned.1.call-update) | async-done | bytes 2097168 | tf_op jit(solution)/shard_map/all_gather | solution.py:87
  325.7 49.2 %while.46 = (s32[]{:T(128)}, f32[1024,1024]{1,0:T(8,128)}, bf16[6,128,1024]{2,1,0:T(8,128)(2,1)}, s32[]{:T(128)}, bf16[6,128,1024]{2,1,0:T(8,128)(2,1)}, /*index...) while((s32[]{:T(128)}, f32[1024,1024]{1,0:T(8,128)}, bf16[6,128,1024]{2,1,0:T(8,128)(2,1)}, ...), condition=%wide.region_14.15_spmd, body=%wide.region_12.14_spmd.sunk | while | flops 807272320 | bytes 14943891 | solution.py:60
  343.8 5.3 %convolution_add_fusion.10 = f32[1024,1024]{1,0:T(8,128)} fusion(f32[1024,1024]{1,0:T(8,128)} %get-tuple-element.406, bf16[6,128,1024]{2,1,0:T(8,128)(2,1)} %get-tuple-element.418, s32[]{:T(128)S(6)} %select_n.47, f32[128,1024]{1,0:T(8,128)S(1)} %get-tuple-element.338, f32[128]{0:T(128)S(1)} %get-tuple-element.339), kind=kOutput, calls=%fused_computation.22.clone.1 | convolution fusion | flops 269746176 | bytes 9175556 | tf_op jit(solution)/shard_map/while/body/dot_general | solution.py:50
  352.2 5.1 %convolution_add_fusion.10 = f32[1024,1024]{1,0:T(8,128)} fusion(f32[1024,1024]{1,0:T(8,128)} %get-tuple-element.406, bf16[6,128,1024]{2,1,0:T(8,128)(2,1)} %get-tuple-element.418, s32[]{:T(128)S(6)} %select_n.47, f32[128,1024]{1,0:T(8,128)S(1)} %get-tuple-element.338, f32[128]{0:T(128)S(1)} %get-tuple-element.339), kind=kOutput, calls=%fused_computation.22.clone.1 | convolution fusion | flops 269746176 | bytes 9175556 | tf_op jit(solution)/shard_map/while/body/dot_general | solution.py:50
  360.4 5.1 %convolution_add_fusion.10 = f32[1024,1024]{1,0:T(8,128)} fusion(f32[1024,1024]{1,0:T(8,128)} %get-tuple-element.406, bf16[6,128,1024]{2,1,0:T(8,128)(2,1)} %get-tuple-element.418, s32[]{:T(128)S(6)} %select_n.47, f32[128,1024]{1,0:T(8,128)S(1)} %get-tuple-element.338, f32[128]{0:T(128)S(1)} %get-tuple-element.339), kind=kOutput, calls=%fused_computation.22.clone.1 | convolution fusion | flops 269746176 | bytes 9175556 | tf_op jit(solution)/shard_map/while/body/dot_general | solution.py:50
  368.5 5.1 %convolution_add_fusion.10 = f32[1024,1024]{1,0:T(8,128)} fusion(f32[1024,1024]{1,0:T(8,128)} %get-tuple-element.406, bf16[6,128,1024]{2,1,0:T(8,128)(2,1)} %get-tuple-element.418, s32[]{:T(128)S(6)} %select_n.47, f32[128,1024]{1,0:T(8,128)S(1)} %get-tuple-element.338, f32[128]{0:T(128)S(1)} %get-tuple-element.339), kind=kOutput, calls=%fused_computation.22.clone.1 | convolution fusion | flops 269746176 | bytes 9175556 | tf_op jit(solution)/shard_map/while/body/dot_general | solution.py:50
  379.3 28.6 %reduce-scatter.11.cloned.1.call-done = f32[64,1024]{1,0:T(8,128)} async-done(((f32[1024,1024]{1,0:T(8,128)}), f32[64,1024]{1,0:T(8,128)}) %reduce-scatter.11.cloned.1.call-update) | async-done | bytes 262160 | tf_op jit(solution)/shard_map/reduce_scatter | solution.py:97
  410.0 5.2 %collective-permute-done.5 = bf16[6,128,1024]{2,1,0:T(8,128)(2,1)} collective-permute-done((bf16[6,128,1024]{2,1,0:T(8,128)(2,1)S(1)}, bf16[6,128,1024]{2,1,0:T(8,128)(2,1)}, u32[]{:S(2)}, u32[]{:S(2)}) %collective-permute-start.5) | collective-permute-done | bytes 1572896 | tf_op jit(solution)/shard_map/ppermute | solution.py:17
  418.5 61.4 %reduce-scatter.9.cloned.1.call-done = f32[64,1024]{1,0:T(8,128)} async-done(((f32[1024,1024]{1,0:T(8,128)}), f32[64,1024]{1,0:T(8,128)}) %reduce-scatter.9.cloned.1.call-update) | async-done | bytes 262160 | tf_op jit(solution)/shard_map/reduce_scatter | solution.py:96
  (103 shorter events, 134.0 us)
Async XLA Ops:
  7.2 10.3 %copy-start.5 = (bf16[1,1536,1024]{2,1,0:T(8,128)(2,1)S(1)}, bf16[1,1536,1024]{2,1,0:T(8,128)(2,1)}, u32[]{:S(2)}) copy-start(bf16[1,1536,1024]{2,1,0:T(8,128)(2,1)} %param.11) | copy-start | bytes 9437188
  7.2 50.3 %all-gather.6.cloned.1.call-start = ((), (), s32[]{:S(2)}) async-start(), calls=%async_computation.5 | async-start | bytes 2228224 | tf_op jit(solution)/shard_map/all_gather | solution.py:89
  7.2 6.9 %collective-permute-start.1 = (bf16[64,1024]{1,0:T(8,128)(2,1)}, bf16[64,1024]{1,0:T(8,128)(2,1)S(1)}, u32[]{:S(2)}, u32[]{:S(2)}) collective-permute-start(bf16[64,1024]{1,0:T(8,128)(2,1)} %bitcast.89), channel_id=1, source_target_pairs={{0,64},{16,80},{32,96},{48,112},{64,0},{80,16},{96,32},{112,48},{1... | collective-permute-start | bytes 393224 | tf_op jit(solution)/shard_map/ppermute | solution.py:17
  14.8 72.1 %all-gather.12.cloned.1.call-start = ((), (), s32[]{:S(2)}) async-start(), calls=%async_computation.11 | async-start | bytes 2228224 | tf_op jit(solution)/shard_map/all_gather | solution.py:87
  18.1 4.8 copy-start.11
  19.5 36.8 %collective-permute-start = (bf16[6,128,1024]{2,1,0:T(8,128)(2,1)S(1)}, bf16[6,128,1024]{2,1,0:T(8,128)(2,1)S(1)}, u32[]{:S(2)}, u32[]{:S(2)}) collective-permute-start(bf16[6,128,1024]{2,1,0:T(8,128)(2,1)S(1)} %bitcast.88), channel_id=1, source_target_pairs={{0,64},{16,80},{32,96},{48,112},{64,0},{80,16},{96,32},{112,48},{1... | collective-permute-start | bytes 4718600 | tf_op jit(solution)/shard_map/ppermute | solution.py:17
  22.8 149.8 %reduce-scatter.7.cloned.1.call-start = ((), (), s32[]{:S(2)}) async-start(), calls=%async_computation.6 | async-start | bytes 4456448 | tf_op jit(solution)/shard_map/reduce_scatter | solution.py:97
  56.3 1.1 copy-start.4
  57.4 2.5 copy-start.2
  80.9 163.7 %reduce-scatter.5.cloned.1.call-start = ((), (), s32[]{:S(2)}) async-start(), calls=%async_computation.4 | async-start | bytes 4456448 | tf_op jit(solution)/shard_map/reduce_scatter | solution.py:96
  87.0 2.5 copy-start
  131.2 154.5 %all-gather.10.cloned.1.call-start = ((), (), s32[]{:S(2)}) async-start(), calls=%async_computation.9 | async-start | bytes 2228224 | tf_op jit(solution)/shard_map/all_gather | solution.py:89
  172.6 72.0 %collective-permute-start.2 = (f32[64,1024]{1,0:T(8,128)}, f32[64,1024]{1,0:T(8,128)S(1)}, u32[]{:S(2)}, u32[]{:S(2)}) collective-permute-start(f32[64,1024]{1,0:T(8,128)} %reduce-scatter.7.cloned.1.call-done), channel_id=1, source_target_pairs={{0,64},{16,80},{32,96},{48,112},{64,0},{80,16},{96,32},{112,48},{1... | collective-permute-start | bytes 786440 | tf_op jit(solution)/shard_map/ppermute | solution.py:17
  245.8 7.3 %copy-start.8 = (bf16[64,1024]{1,0:T(8,128)(2,1)}, bf16[64,1024]{1,0:T(8,128)(2,1)S(1)}, u32[]{:S(2)}) copy-start(bf16[64,1024]{1,0:T(8,128)(2,1)S(1)} %multiply_convert_fusion) | copy-start | bytes 393220
  245.8 6.6 %collective-permute-start.3 = (bf16[64,1024]{1,0:T(8,128)(2,1)S(1)}, bf16[64,1024]{1,0:T(8,128)(2,1)S(1)}, u32[]{:S(2)}, u32[]{:S(2)}) collective-permute-start(bf16[64,1024]{1,0:T(8,128)(2,1)S(1)} %multiply_convert_fusion), channel_id=1, source_target_pairs={{0,64},{16,80},{32,96},{48,112},{64,0},{80,16},{96,32},{112,48},{1... | collective-permute-start | bytes 393224 | tf_op jit(solution)/shard_map/ppermute | solution.py:17
  253.0 68.8 %all-gather.8.cloned.1.call-start = ((), (), s32[]{:S(2)}) async-start(), calls=%async_computation.7 | async-start | bytes 2228224 | tf_op jit(solution)/shard_map/all_gather | solution.py:87
  253.6 154.3 %reduce-scatter.11.cloned.1.call-start = ((), (), s32[]{:S(2)}) async-start(), calls=%async_computation.10 | async-start | bytes 4456448 | tf_op jit(solution)/shard_map/reduce_scatter | solution.py:97
  285.8 3.9 copy-start.3
  314.2 165.7 %reduce-scatter.9.cloned.1.call-start = ((), (), s32[]{:S(2)}) async-start(), calls=%async_computation.8 | async-start | bytes 4456448 | tf_op jit(solution)/shard_map/reduce_scatter | solution.py:96
  321.8 3.8 copy-start.1
  374.9 1.4 copy-start.7
  374.9 40.3 %copy-start.6 = (bf16[6,128,1024]{2,1,0:T(8,128)(2,1)S(1)}, bf16[6,128,1024]{2,1,0:T(8,128)(2,1)}, u32[]{:S(2)}) copy-start(bf16[6,128,1024]{2,1,0:T(8,128)(2,1)} %get-tuple-element.130) | copy-start | bytes 4718596
  376.3 38.9 %collective-permute-start.5 = (bf16[6,128,1024]{2,1,0:T(8,128)(2,1)S(1)}, bf16[6,128,1024]{2,1,0:T(8,128)(2,1)}, u32[]{:S(2)}, u32[]{:S(2)}) collective-permute-start(bf16[6,128,1024]{2,1,0:T(8,128)(2,1)S(1)} %copy-done.7), channel_id=1, source_target_pairs={{0,64},{16,80},{32,96},{48,112},{64,0},{80,16},{96,32},{112,48},{1... | collective-permute-start | bytes 4718600 | tf_op jit(solution)/shard_map/ppermute | solution.py:17
  407.9 72.0 %collective-permute-start.4 = (f32[64,1024]{1,0:T(8,128)}, f32[64,1024]{1,0:T(8,128)S(1)}, u32[]{:S(2)}, u32[]{:S(2)}) collective-permute-start(f32[64,1024]{1,0:T(8,128)} %reduce-scatter.11.cloned.1.call-done), channel_id=1, source_target_pairs={{0,64},{16,80},{32,96},{48,112},{64,0},{80,16},{96,32},{112,48},{1... | collective-permute-start | bytes 786440 | tf_op jit(solution)/shard_map/ppermute | solution.py:17
  (2 other events, 1.3 us)
Sparse Core Ops, SparseCore 0:
  14.9 36.5 all-gather.5
  53.2 33.7 all-gather.11
  89.4 83.1 reduce-scatter.6
  174.8 69.7 reduce-scatter.4
  253.2 32.5 all-gather.9
  287.9 33.8 all-gather.7
  324.2 83.5 reduce-scatter.10
  410.3 69.5 reduce-scatter.8
where the time goes:
time: 491 us; the launch traced here: 489 us
  waiting for transfers between devices  291 us (59%)
  matrix products  136 us (28%)
  local copies, waits for them, and re-layouts  18 us (4%)
  starting transfers between devices  17.8 us (4%)
  between operations  15.6 us (3%)
  other arithmetic  10.2 us (2%)
    reduce_scatter x2, waiting for transfers between devices, body(): lax.psum_scatter(own_total, 'shard', scatter_dimension=0, tiled=True)  130 us
    dot_general x18, matrix products, visit(): lax.dot_general(weights, rows_per_tile, (((0,), (0,)), ((), ())), preferr...  91.8 us
    reduce_scatter x2, waiting for transfers between devices, body(): lax.psum_scatter(lent_total, 'shard', scatter_dimension=0, tiled=True)  69.9 us
    ppermute x6, waiting for transfers between devices, partner(): return lax.ppermute(value, axis, pairs)  44.6 us
    dot_general x18, matrix products, tile_weights(): lax.dot_general(rows_per_tile, centroid_table, (((1,), (1,)), ((), ())),...  33.7 us
    all_gather x2, waiting for transfers between devices, body(): lent_table = lax.all_gather(lent_piece, 'shard', axis=0, tiled=True)  32.1 us
    ppermute x6, starting transfers between devices, partner(): return lax.ppermute(value, axis, pairs)  17.5 us
    all_gather x2, waiting for transfers between devices, body(): centroid_table = lax.all_gather(current_shard, 'shard', axis=0, tiled=True)  12.9 us
  transfers between devices with their start and end apart: 14, of which 11 were waited for; matrix products, arithmetic and copies ran while one was open for 32% of the time, Pallas kernels for 0%

commit v1 on v0

v1 whole, which is shorter than its diff:
```python
import functools
import math

import jax
import jax.numpy as jnp
from jax import lax
from jax.experimental import pallas as pl
from jax.experimental.pallas import tpu as pltpu
from jax.sharding import PartitionSpec as P

MESH = pl.DeviceIdType.MESH
TILE = 128
ITERS = 2
EPS = 1e-06
SHARP = 48.0
Q = 2
F32 = jnp.float32
BF16 = jnp.bfloat16
N_SEMS = 128


def kernel(
    counts, points, cents, newc, post,
    pts, n, e, den, inv, tab, acc, ssnd, srcv, x, r1, r2, r3, ctr, pout,
    send, recv, lsem,
):
    rows_all, width = n.shape
    per = tab.shape[4]
    half = per // 2
    g = lax.axis_index("grp")
    sh = lax.axis_index("shard")
    z, y, c = sh // 4, (sh // 2) % 2, sh % 2

    def peer(dz, dy, dc):
        zz = (z + dz) % 4
        yy = (y + dy) % 2
        cc = (c + dc) % 2
        return (g, zz * 4 + yy * 2 + cc)

    zp, zm, yo, sib = peer(1, 0, 0), peer(3, 0, 0), peer(0, 1, 0), peer(0, 0, 1)

    copies = {}

    def start(key, src, dst, dev):
        i = len(copies)
        cp = pltpu.make_async_remote_copy(
            src_ref=src, dst_ref=dst, send_sem=send.at[i], recv_sem=recv.at[i],
            device_id=dev, device_id_type=MESH,
        )
        cp.start()
        copies[key] = cp

    def got(*key):
        copies[key].wait_recv()

    parts = 4
    prow = rows_all // parts
    loads = []
    for i in range(parts):
        cp = pltpu.make_async_copy(
            points.at[0, pl.ds(i * prow, prow)], pts.at[pl.ds(i * prow, prow)], lsem.at[i]
        )
        cp.start()
        loads.append(cp)
    own_loads = []
    for q in range(Q):
        cp = pltpu.make_async_copy(
            cents.at[0, pl.ds(q * per, per)], tab.at[0, 0, q, 0], lsem.at[parts + q]
        )
        cp.start()
        own_loads.append(cp)

    barrier = pltpu.get_barrier_semaphore()
    for dev in (zp, zm, yo, sib):
        pl.semaphore_signal(barrier, inc=1, device_id=dev, device_id_type=MESH)
    pl.semaphore_wait(barrier, 4)

    def ag_own(it, q, src):
        start((it, q, "zp"), src, tab.at[it, 3, q, 0], zp)
        start((it, q, "zm"), src, tab.at[it, 2, q, 0], zm)
        start((it, q, "y"), src, tab.at[it, 1, q, 0], yo)
        start((it, q, "s0"), src, tab.at[it, 0, q, 1], sib)

    def ag_relay_a(it, q):
        got(it, q, "zp")
        start((it, q, "hzp"), tab.at[it, 3, q, 0, pl.ds(0, half)], tab.at[it, 4, q, 0, pl.ds(0, half)], zp)
        got(it, q, "zm")
        start((it, q, "hzm"), tab.at[it, 2, q, 0, pl.ds(half, half)], tab.at[it, 4, q, 0, pl.ds(half, half)], zm)
        got(it, q, "y")
        start((it, q, "s1"), tab.at[it, pl.ds(1, 3), q, 0], tab.at[it, pl.ds(1, 3), q, 1], sib)

    def ag_relay_b(it, q):
        start((it, q, "yzp"), tab.at[it, 1, q, 0], tab.at[it, 6, q, 0], zp)
        start((it, q, "yzm"), tab.at[it, 1, q, 0], tab.at[it, 5, q, 0], zm)

    def ag_relay_c(it, q):
        got(it, q, "hzp")
        got(it, q, "hzm")
        start((it, q, "hy"), tab.at[it, 4, q, 0], tab.at[it, 7, q, 0], yo)
        start((it, q, "s2"), tab.at[it, 4, q, 0], tab.at[it, 4, q, 1], sib)

    def ag_relay_d(it, q):
        got(it, q, "yzp")
        got(it, q, "yzm")
        got(it, q, "hy")
        start((it, q, "s3"), tab.at[it, pl.ds(5, 3), q, 0], tab.at[it, pl.ds(5, 3), q, 1], sib)

    scale = SHARP / width * math.log2(math.e)

    def logits(it, p0, p1, q0, q1, first=False):
        m = (p1 - p0) * (q1 - q0) * 2 * per

        def step(rt, carry):
            at = pl.ds(pl.multiple_of(rt * 256, 256), 256)
            s = lax.dot_general(
                tab[it, p0:p1, q0:q1].reshape(m, width), n[at, :],
                (((1,), (1,)), ((), ())), preferred_element_type=F32,
            )
            ex = jnp.exp2(s * scale)
            part = jnp.sum(ex.reshape(m // 8, 8, 256), axis=0)
            den[:, at] = part if first else den[:, at] + part
            e[p0:p1, q0:q1, :, :, at] = ex.astype(BF16).reshape(p1 - p0, q1 - q0, 2, per, 256)
            return carry

        lax.fori_loop(0, rows_all // 256, step, 0)

    def invert():
        for t in range(rows_all // TILE):
            at = slice(t * TILE, (t + 1) * TILE)
            live = (t * 16 + sh < counts[g]).astype(F32)
            inv[:, at] = live / jnp.sum(den[:, at], axis=0, keepdims=True)

    def weigh(p0, p1, q0, q1):
        m = (p1 - p0) * (q1 - q0) * 2 * per

        def step(j, carry):
            at = pl.ds(pl.multiple_of(j * 256, 256), 256)
            v = e[p0:p1, q0:q1, :, :, at].reshape(m, 256).astype(F32) * inv[:, at]
            e[p0:p1, q0:q1, :, :, at] = v.astype(BF16).reshape(p1 - p0, q1 - q0, 2, per, 256)
            return carry

        lax.fori_loop(0, rows_all // 256, step, 0)

    def sums(it, p0, p1, q0, q1):
        weigh(p0, p1, q0, q1)
        m = (p1 - p0) * (q1 - q0) * 2 * per

        def step(ft, carry):
            at = pl.ds(pl.multiple_of(ft * 256, 256), 256)
            s = jnp.dot(
                e[p0:p1, q0:q1].reshape(m, rows_all), n[:, at], preferred_element_type=F32
            ).reshape(p1 - p0, q1 - q0, 2, per, 256)
            acc[p0:p1, q0:q1, :, at] = s[:, :, 0]
            ssnd[it, p0:p1, q0:q1, :, at] = s[:, :, 1].astype(BF16)
            return carry

        lax.fori_loop(0, width // 256, step, 0)
        for q in range(q0, q1):
            start((it, q, "x", p0), ssnd.at[it, pl.ds(p0, p1 - p0), q], srcv.at[it, pl.ds(p0, p1 - p0), q], sib)

    def base(it, p, q, rows=slice(None)):
        return acc[p, q, rows] + srcv[it, p, q, rows].astype(F32)

    def rs_one(it, q):
        got(it, q, "x", 5)
        for p, dev in ((5, zp), (6, zm), (7, yo)):
            x[it, p, q] = base(it, p, q).astype(BF16)
            start((it, q, "r1", p - 5), x.at[it, p, q], r1.at[it, p - 5, q], dev)

    lo, hi = slice(0, half), slice(half, 2 * half)

    def rs_two(it, q):
        got(it, q, "x", 2)
        got(it, q, "r1", 2)
        x[it, 4, q] = (base(it, 4, q) + r1[it, 2, q].astype(F32)).astype(BF16)
        start((it, q, "r2", 0), x.at[it, 4, q, pl.ds(0, half)], r2.at[it, 0, q], zm)
        start((it, q, "r2", 1), x.at[it, 4, q, pl.ds(half, half)], r2.at[it, 1, q], zp)
        got(it, q, "x", 0)
        got(it, q, "r1", 0)
        got(it, q, "r1", 1)
        x[it, 1, q] = (base(it, 1, q) + r1[it, 0, q].astype(F32) + r1[it, 1, q].astype(F32)).astype(BF16)
        start((it, q, "r3", 2), x.at[it, 1, q], r3.at[it, 2, q], yo)
        x[it, 3, q, hi] = base(it, 3, q, hi).astype(BF16)
        start((it, q, "r3e", 0), x.at[it, 3, q, pl.ds(half, half)], r3.at[it, 0, q, pl.ds(half, half)], zm)
        x[it, 2, q, lo] = base(it, 2, q, lo).astype(BF16)
        start((it, q, "r3e", 1), x.at[it, 2, q, pl.ds(0, half)], r3.at[it, 1, q, pl.ds(0, half)], zp)

    def rs_three(it, q):
        got(it, q, "r2", 0)
        x[it, 3, q, lo] = (base(it, 3, q, lo) + r2[it, 0, q].astype(F32)).astype(BF16)
        start((it, q, "r3", 0), x.at[it, 3, q, pl.ds(0, half)], r3.at[it, 0, q, pl.ds(0, half)], zm)
        got(it, q, "r2", 1)
        x[it, 2, q, hi] = (base(it, 2, q, hi) + r2[it, 1, q].astype(F32)).astype(BF16)
        start((it, q, "r3", 1), x.at[it, 2, q, pl.ds(half, half)], r3.at[it, 1, q, pl.ds(half, half)], zp)

    def rs_last(it, q):
        for key in (("r3", 2), ("r3e", 0), ("r3e", 1), ("r3", 0), ("r3", 1)):
            got(it, q, *key)
        s = base(it, 0, q)
        for i in range(3):
            s = s + r3[it, i, q].astype(F32)
        s = s * lax.rsqrt(jnp.mean(s * s, axis=-1, keepdims=True) + EPS)
        return s

    def post_tiles(t0, t1):
        def step(t, carry):
            at = pl.ds(pl.multiple_of(t * 256, 256), 256)
            w = e[:, :, :, :, at].reshape(16 * Q * per, 256)
            pout[at, :] = lax.dot_general(
                w, tab[ITERS - 1].reshape(16 * Q * per, width),
                (((0,), (0,)), ((), ())), preferred_element_type=F32,
            ).astype(BF16)
            return carry

        lax.fori_loop(t0, t1, step, 0)
        cp = pltpu.make_async_copy(
            pout.at[pl.ds(t0 * 256, (t1 - t0) * 256)],
            post.at[0, pl.ds(t0 * 256, (t1 - t0) * 256)], lsem.at[parts + Q + t0],
        )
        cp.start()
        return cp

    for q in range(Q):
        ag_own(0, q, cents.at[0, pl.ds(q * per, per)])

    def unit(j, carry):
        at = pl.ds(pl.multiple_of(j * 32, 32), 32)
        v = pts[at, :].astype(F32)
        n[at, :] = (v * lax.rsqrt(jnp.mean(v * v, axis=-1, keepdims=True) + EPS)).astype(BF16)
        return carry

    for i in range(parts):
        loads[i].wait()
        lax.fori_loop(i * prow // 32, (i + 1) * prow // 32, unit, 0)
    for cp in own_loads:
        cp.wait()

    outs = []
    for it in range(ITERS):
        last = it == ITERS - 1
        for q in range(Q):
            got(it, q, "s0")
        logits(it, 0, 1, 0, Q, first=True)
        for q in range(Q):
            ag_relay_a(it, q)
        for q in range(Q):
            ag_relay_b(it, q)
        for q in range(Q):
            got(it, q, "s1")
        logits(it, 1, 4, 0, Q)
        for q in range(Q):
            ag_relay_c(it, q)
        for q in range(Q):
            ag_relay_d(it, q)
            got(it, q, "s2")
            got(it, q, "s3")
            logits(it, 4, 8, q, q + 1)
        invert()
        for q in range(Q):
            sums(it, 5, 8, q, q + 1)
        for q in range(Q):
            sums(it, 2, 5, q, q + 1)
            rs_one(it, q)
        sums(it, 0, 2, 0, Q)
        if last:
            outs.append(post_tiles(0, 2))
        for q in range(Q):
            rs_two(it, q)
            if last:
                outs.append(post_tiles(2 + q, 3 + q))
        if last:
            outs.append(post_tiles(4, 6))
        for q in range(Q):
            rs_three(it, q)
        for q in range(Q):
            s = rs_last(it, q)
            if last:
                ctr[q] = s
                cp = pltpu.make_async_copy(
                    ctr.at[q], newc.at[0, pl.ds(q * per, per)], lsem.at[parts + q]
                )
                cp.start()
                outs.append(cp)
            else:
                tab[it + 1, 0, q, 0] = s.astype(BF16)
                ag_own(it + 1, q, tab.at[it + 1, 0, q, 0])
    for cp in copies.values():
        cp.wait_send()
    for cp in outs:
        cp.wait()


def body(points, centroids, tile_counts):
    rows, width = points.shape[1:]
    mine = centroids.shape[1]
    k = mine * 16
    per = mine // Q
    dma = pltpu.SemaphoreType.DMA
    scratch = [
        pltpu.VMEM((rows, width), BF16),
        pltpu.VMEM((rows, width), BF16),
        pltpu.VMEM((8, Q, 2, per, rows), BF16),
        pltpu.VMEM((8, rows), F32),
        pltpu.VMEM((1, rows), F32),
        pltpu.VMEM((ITERS, 8, Q, 2, per, width), BF16),
        pltpu.VMEM((8, Q, per, width), F32),
        pltpu.VMEM((ITERS, 8, Q, per, width), BF16),
        pltpu.VMEM((ITERS, 8, Q, per, width), BF16),
        pltpu.VMEM((ITERS, 8, Q, per, width), BF16),
        pltpu.VMEM((ITERS, 3, Q, per, width), BF16),
        pltpu.VMEM((ITERS, 2, Q, per // 2, width), BF16),
        pltpu.VMEM((ITERS, 3, Q, per, width), BF16),
        pltpu.VMEM((Q, per, width), F32),
        pltpu.VMEM((rows, width), BF16),
        dma((N_SEMS,)), dma((N_SEMS,)), dma((16,)),
    ]
    anyspace = pl.BlockSpec(memory_space=pl.ANY)
    return pl.pallas_call(
        kernel,
        out_shape=(
            jax.ShapeDtypeStruct((1, mine, width), F32),
            jax.ShapeDtypeStruct((1, rows, width), BF16),
        ),
        in_specs=[pl.BlockSpec(memory_space=pltpu.SMEM), anyspace, anyspace],
        out_specs=(anyspace, anyspace),
        scratch_shapes=scratch,
        compiler_params=pltpu.CompilerParams(
            collective_id=0, has_side_effects=True, vmem_limit_bytes=60 * 1024 * 1024
        ),
    )(tile_counts, points, centroids)


def solution(mesh):
    return jax.shard_map(
        body,
        mesh=mesh,
        in_specs=(P("grp", "shard", None), P("grp", "shard", None), P()),
        out_specs=(P("grp", "shard", None), P("grp", "shard", None)),
        check_vma=False,
    )
```

time: 491 us -> 88.4 us (0.18)
  waiting for transfers between devices: 291 us -> 0 us
  matrix products: 136 us -> 0 us
  Pallas kernels: 0 us -> 82.1 us
  starting transfers between devices: 17.8 us -> 0 us
  between operations: 15.6 us -> 0.64 us
  local copies, waits for them, and re-layouts: 18 us -> 5.53 us
  other arithmetic: 10.2 us -> 0 us
    reduce_scatter x4 -> x0, waiting for transfers between devices: 200 us -> none  [the longest x2 130 us: body(): lax.psum_scatter(own_total, 'shard', scatter_dimension=0, tiled=True)]
    dot_general x45 -> x0, matrix products: 136 us -> none  [the longest x18 91.8 us: visit(): lax.dot_general(weights, rows_per_tile, (((0,), (0,)), ((), ())), preferr...]
    pallas_call x0 -> x1, Pallas kernels: none -> 82.1 us  [body(): pl.pallas_call(kernel, out_shape=(jax.ShapeDtypeStruct((1, mine, width),...]
    all_gather x4 -> x0, waiting for transfers between devices: 45 us -> none  [the longest x2 32.1 us: body(): lent_table = lax.all_gather(lent_piece, 'shard', axis=0, tiled=True)]
    ppermute x6 -> x0, waiting for transfers between devices: 44.6 us -> none  [partner(): return lax.ppermute(value, axis, pairs)]
    ppermute x6 -> x0, starting transfers between devices: 17.5 us -> none  [partner(): return lax.ppermute(value, axis, pairs)]
    another operation x6 -> x0, local copies, waits for them, and re-layouts: 12.7 us -> none
    reduce_sum x4 -> x0, other arithmetic: 5.4 us -> none  [the longest x3 4.73 us: rms_unit(): jnp.mean(values * values, axis=-1, keepdims=True) + epsilon]
  transfers between devices with their start and end apart: 14 -> 0, of which waited for: 11 -> 0; matrix products, arithmetic and copies ran while one was open for 32% -> 0% of each run, Pallas kernels for 0% -> 0%
where the time goes in v1:
time: 88.4 us; the launch traced here: 88.2 us
  Pallas kernels  82.1 us (93%)
  local copies, waits for them, and re-layouts  5.53 us (6%)
    pallas_call x1, Pallas kernels, body(): pl.pallas_call(kernel, out_shape=(jax.ShapeDtypeStruct((1, mine, width),...  82.1 us
    unnamed x2, local copies, waits for them, and re-layouts  5.53 us

profile of v1, /device:TPU:0, one launch (start us, length us, event | category | flops | bytes accessed | tf_op | source)
XLA Modules:
  0.0 88.2 jit_solution(1744859127348610665)
XLA Ops:
  0.6 82.1 %shard_map.50 = (f32[1,64,1024]{2,1,0:T(8,128)}, bf16[1,1536,1024]{2,1,0:T(8,128)(2,1)}) custom-call(s32[8]{0:T(128)} %counts.1, bf16[1,1536,1024]{2,1,0:T(8,128)(2,1)} %points.1, bf16[1,64,1024]{2,1,0:T(8,128)(2,1)} %cents.1), custom_call_target="tpu_custom_call" | custom-call | tf_op jit(solution)/shard_map/pallas_call | solution.py:318
  82.7 1.7 %copy.7 = f32[1,64,1024]{2,1,0:T(8,128)} copy(f32[1,64,1024]{2,1,0:T(8,128)} %get-tuple-element.4) | data formatting | bytes 524288
  84.4 3.9 %copy.8 = bf16[1,1536,1024]{2,1,0:T(8,128)(2,1)} copy(bf16[1,1536,1024]{2,1,0:T(8,128)(2,1)} %get-tuple-element.5) | data formatting | bytes 6291456

commit v2 on v1

v2 whole, which is shorter than its diff:
```python
import math

import jax
import jax.numpy as jnp
from jax import lax
from jax.experimental import pallas as pl
from jax.experimental.pallas import tpu as pltpu
from jax.sharding import PartitionSpec as P

MESH = pl.DeviceIdType.MESH
TILE = 128
ITERS = 2
EPS = 1e-06
SHARP = 48.0
Q = 4
F32 = jnp.float32
BF16 = jnp.bfloat16
N_SEMS = 192
VLIM = 30
UNROLL = 2
YO, ZP1, ZM1, OWN, ZZ = 0, 1, 2, 3, 4


def kernel(
    counts_in, points, cents, newc, post,
    counts, pts, n, e, den, inv, tab, acc, ssnd, srcv, x, r1, r2, r3, ctr, pout,
    send, recv, lsem,
):
    rows_all, width = n.shape
    per = tab.shape[4]
    g = lax.axis_index("grp")
    sh = lax.axis_index("shard")
    z, y, c = sh // 4, (sh // 2) % 2, sh % 2

    def peer(dz, dy, dc):
        zz = (z + dz) % 4
        yy = (y + dy) % 2
        cc = (c + dc) % 2
        return (g, zz * 4 + yy * 2 + cc)

    zp, zm, yo, sib = peer(1, 0, 0), peer(3, 0, 0), peer(0, 1, 0), peer(0, 0, 1)

    copies = {}
    drained = set()

    def start(key, src, dst, dev):
        i = len(copies)
        cp = pltpu.make_async_remote_copy(
            src_ref=src, dst_ref=dst, send_sem=send.at[i], recv_sem=recv.at[i],
            device_id=dev, device_id_type=MESH,
        )
        cp.start()
        copies[key] = cp

    def got(*key):
        copies[key].wait_recv()

    def drain():
        for key, cp in copies.items():
            if key not in drained:
                cp.wait_send()
                drained.add(key)

    parts = 4
    prow = rows_all // parts
    loads = []
    for i in range(parts):
        cp = pltpu.make_async_copy(
            points.at[0, pl.ds(i * prow, prow)], pts.at[pl.ds(i * prow, prow)], lsem.at[i]
        )
        cp.start()
        loads.append(cp)
    for q in range(Q):
        cp = pltpu.make_async_copy(
            cents.at[0, pl.ds(q * per, per)], tab.at[0, OWN, q, 0], lsem.at[parts + q]
        )
        cp.start()
        loads.append(cp)

    cp = pltpu.make_async_copy(counts_in, counts, lsem.at[15])
    cp.start()
    loads.append(cp)

    barrier = pltpu.get_barrier_semaphore()
    for dev in (zp, zm, yo, sib):
        pl.semaphore_signal(barrier, inc=1, device_id=dev, device_id_type=MESH)
    pl.semaphore_wait(barrier, 4)

    def ag_own(it, q, src):
        start((it, q, "zp"), src, tab.at[it, ZM1, q, 0], zp)
        start((it, q, "zm"), src, tab.at[it, ZP1, q, 0], zm)
        start((it, q, "y"), src, tab.at[it, YO, q, 0], yo)
        start((it, q, "s0"), src, tab.at[it, OWN, q, 1], sib)

    def ag_a(it, q):
        got(it, q, "zp")
        if q % 2 == 0:
            start((it, q, "h"), tab.at[it, ZM1, q, 0], tab.at[it, ZZ, q, 0], zp)
        got(it, q, "zm")
        if q % 2 == 1:
            start((it, q, "h"), tab.at[it, ZP1, q, 0], tab.at[it, ZZ, q, 0], zm)
        got(it, q, "y")
        start((it, q, "s1"), tab.at[it, pl.ds(0, 3), q, 0], tab.at[it, pl.ds(0, 3), q, 1], sib)

    def ag_b(it, q):
        start((it, q, "yzp"), tab.at[it, YO, q, 0], tab.at[it, 6, q, 0], zp)
        start((it, q, "yzm"), tab.at[it, YO, q, 0], tab.at[it, 5, q, 0], zm)

    def ag_c(it, q):
        got(it, q, "h")
        start((it, q, "hy"), tab.at[it, ZZ, q, 0], tab.at[it, 7, q, 0], yo)
        start((it, q, "s2"), tab.at[it, ZZ, q, 0], tab.at[it, ZZ, q, 1], sib)

    def ag_d(it, q):
        got(it, q, "yzp")
        got(it, q, "yzm")
        start((it, q, "s3"), tab.at[it, pl.ds(5, 2), q, 0], tab.at[it, pl.ds(5, 2), q, 1], sib)

    def ag_e(it, q):
        got(it, q, "hy")
        start((it, q, "s4"), tab.at[it, 7, q, 0], tab.at[it, 7, q, 1], sib)

    scale = SHARP / width * math.log2(math.e)
    n_rt = rows_all // 256

    def logits(it, p0, p1, q0, q1, t0=0, t1=n_rt, first=False):
        m = (p1 - p0) * (q1 - q0) * 2 * per

        def step(rt, carry):
            at = pl.ds(pl.multiple_of(rt * 256, 256), 256)
            s = lax.dot_general(
                tab[it, p0:p1, q0:q1].reshape(m, width), n[at, :],
                (((1,), (1,)), ((), ())), preferred_element_type=F32,
            )
            ex = jnp.exp2(s * scale)
            part = jnp.sum(ex.reshape(m // 8, 8, 256), axis=0)
            den[:, at] = part if first else den[:, at] + part
            e[p0:p1, q0:q1, :, :, at] = ex.astype(BF16).reshape(p1 - p0, q1 - q0, 2, per, 256)
            return carry

        lax.fori_loop(t0, t1, step, 0, unroll=UNROLL)

    def invert():
        for t in range(rows_all // TILE):
            at = slice(t * TILE, (t + 1) * TILE)
            live = (t * 16 + sh < counts[g]).astype(F32)
            inv[:, at] = live / jnp.sum(den[:, at], axis=0, keepdims=True)

    def sums(it, p0, p1, q0, q1):
        m = (p1 - p0) * (q1 - q0) * 2 * per

        def weigh(j, carry):
            at = pl.ds(pl.multiple_of(j * 256, 256), 256)
            v = e[p0:p1, q0:q1, :, :, at].reshape(m, 256).astype(F32) * inv[:, at]
            e[p0:p1, q0:q1, :, :, at] = v.astype(BF16).reshape(p1 - p0, q1 - q0, 2, per, 256)
            return carry

        lax.fori_loop(0, n_rt, weigh, 0, unroll=UNROLL)

        def step(ft, carry):
            at = pl.ds(pl.multiple_of(ft * 256, 256), 256)
            s = jnp.dot(
                e[p0:p1, q0:q1].reshape(m, rows_all), n[:, at], preferred_element_type=F32
            ).reshape(p1 - p0, q1 - q0, 2, per, 256)
            acc[p0:p1, q0:q1, :, at] = s[:, :, 0]
            ssnd[it, p0:p1, q0:q1, :, at] = s[:, :, 1].astype(BF16)
            return carry

        lax.fori_loop(0, width // 256, step, 0, unroll=UNROLL)
        for q in range(q0, q1):
            start((it, q, "x", p0), ssnd.at[it, pl.ds(p0, p1 - p0), q], srcv.at[it, pl.ds(p0, p1 - p0), q], sib)

    def base(it, p, q):
        return acc[p, q] + srcv[it, p, q].astype(F32)

    def rs_one(it, q):
        got(it, q, "x", 5)
        for p, dev in ((5, zp), (6, zm), (7, yo)):
            x[it, p, q] = base(it, p, q).astype(BF16)
            start((it, q, "r1", p - 5), x.at[it, p, q], r1.at[it, p - 5, q], dev)

    def rs_two(it, q):
        got(it, q, "x", 3)
        got(it, q, "r1", 2)
        x[it, ZZ, q] = (base(it, ZZ, q) + r1[it, 2, q].astype(F32)).astype(BF16)
        start((it, q, "r2"), x.at[it, ZZ, q], r2.at[it, q], zm if q % 2 == 0 else zp)

    def rs_early(it, q):
        got(it, q, "x", 0)
        p, slot, dev = (ZP1, 1, zp) if q % 2 == 0 else (ZM1, 0, zm)
        x[it, p, q] = base(it, p, q).astype(BF16)
        start((it, q, "r3", slot), x.at[it, p, q], r3.at[it, slot, q], dev)

    def rs_y(it, q):
        got(it, q, "r1", 0)
        got(it, q, "r1", 1)
        x[it, YO, q] = (base(it, YO, q) + r1[it, 0, q].astype(F32) + r1[it, 1, q].astype(F32)).astype(BF16)
        start((it, q, "r3", 2), x.at[it, YO, q], r3.at[it, 2, q], yo)

    def rs_three(it, q):
        got(it, q, "r2")
        p, slot, dev = (ZM1, 0, zm) if q % 2 == 0 else (ZP1, 1, zp)
        x[it, p, q] = (base(it, p, q) + r2[it, q].astype(F32)).astype(BF16)
        start((it, q, "r3", slot), x.at[it, p, q], r3.at[it, slot, q], dev)

    def rs_last(it, q):
        s = base(it, OWN, q)
        for i in range(3):
            got(it, q, "r3", i)
            s = s + r3[it, i, q].astype(F32)
        return s * lax.rsqrt(jnp.mean(s * s, axis=-1, keepdims=True) + EPS)

    outs = []

    def post_tile(t):
        at = slice(t * 256, (t + 1) * 256)
        w = e[:, :, :, :, at].reshape(16 * Q * per, 256)
        pout[at, :] = lax.dot_general(
            w, tab[ITERS - 1].reshape(16 * Q * per, width),
            (((0,), (0,)), ((), ())), preferred_element_type=F32,
        ).astype(BF16)
        cp = pltpu.make_async_copy(
            pout.at[pl.ds(t * 256, 256)], post.at[0, pl.ds(t * 256, 256)], lsem.at[parts + Q + t]
        )
        cp.start()
        outs.append(cp)

    for q in range(Q):
        ag_own(0, q, cents.at[0, pl.ds(q * per, per)])

    def unit(j, carry):
        at = pl.ds(pl.multiple_of(j * 32, 32), 32)
        v = pts[at, :].astype(F32)
        n[at, :] = (v * lax.rsqrt(jnp.mean(v * v, axis=-1, keepdims=True) + EPS)).astype(BF16)
        return carry

    for i in range(parts):
        loads[i].wait()
        lax.fori_loop(i * prow // 32, (i + 1) * prow // 32, unit, 0, unroll=2)
    for cp in loads[parts:]:
        cp.wait()

    for it in range(ITERS):
        last = it == ITERS - 1
        if it > 0:
            drain()
        ag_a(it, 0)
        ag_b(it, 0)
        ag_a(it, 1)
        ag_a(it, 2)
        ag_b(it, 1)
        ag_a(it, 3)
        ag_b(it, 2)
        ag_b(it, 3)
        got(it, 0, "s1")
        got(it, 1, "s1")
        logits(it, 0, 3, 0, 2, first=True)
        ag_c(it, 0)
        ag_c(it, 1)
        got(it, 2, "s1")
        got(it, 3, "s1")
        logits(it, 0, 3, 2, 4, 0, 4)
        ag_c(it, 2)
        logits(it, 0, 3, 2, 4, 4, 6)
        ag_c(it, 3)
        ag_d(it, 0)
        ag_d(it, 1)
        ag_e(it, 0)
        for q in range(Q):
            got(it, q, "s0")
            got(it, q, "s2")
        logits(it, 3, 5, 0, 4, 0, 2)
        ag_e(it, 1)
        ag_d(it, 2)
        logits(it, 3, 5, 0, 4, 2, 4)
        ag_e(it, 2)
        ag_d(it, 3)
        logits(it, 3, 5, 0, 4, 4, 6)
        for q in range(2):
            got(it, q, "s3")
            got(it, q, "s4")
        logits(it, 5, 8, 0, 2, 0, 2)
        ag_e(it, 3)
        logits(it, 5, 8, 0, 2, 2, 6)
        for q in range(2, 4):
            got(it, q, "s3")
            got(it, q, "s4")
        logits(it, 5, 8, 2, 4)
        invert()

        def fill(t):
            if last:
                post_tile(t)

        sums(it, 5, 8, 0, 2)
        sums(it, 5, 8, 2, 4)
        rs_one(it, 0)
        rs_one(it, 1)
        sums(it, 3, 5, 0, 4)
        rs_one(it, 2)
        rs_one(it, 3)
        sums(it, 0, 3, 0, 2)
        rs_two(it, 0)
        rs_two(it, 1)
        sums(it, 0, 3, 2, 4)
        rs_two(it, 2)
        rs_early(it, 0)
        rs_early(it, 1)
        rs_y(it, 0)
        rs_two(it, 3)
        rs_y(it, 1)
        rs_early(it, 2)
        rs_early(it, 3)
        fill(0)
        rs_three(it, 0)
        rs_y(it, 2)
        rs_y(it, 3)
        fill(1)
        rs_three(it, 1)
        fill(2)
        rs_three(it, 2)
        fill(3)
        rs_three(it, 3)
        fill(4)
        fill(5)
        for q in range(Q):
            s = rs_last(it, q)
            if last:
                ctr[q] = s
                cp = pltpu.make_async_copy(
                    ctr.at[q], newc.at[0, pl.ds(q * per, per)], lsem.at[parts + q]
                )
                cp.start()
                outs.append(cp)
            else:
                tab[it + 1, OWN, q, 0] = s.astype(BF16)
                ag_own(it + 1, q, tab.at[it + 1, OWN, q, 0])
    drain()
    for cp in outs:
        cp.wait()


def flush(newc_in, post_in, newc, post, sems):
    rows = post.shape[1]
    parts = 4
    cut = rows // parts
    cps = [pltpu.make_async_copy(newc_in, newc, sems.at[parts])]
    for i in range(parts):
        at = pl.ds(i * cut, cut)
        cps.append(pltpu.make_async_copy(post_in.at[0, at], post.at[0, at], sems.at[i]))
    for cp in cps:
        cp.start()
    for cp in cps:
        cp.wait()


def body(points, centroids, tile_counts):
    rows, width = points.shape[1:]
    mine = centroids.shape[1]
    per = mine // Q
    dma = pltpu.SemaphoreType.DMA
    scratch = [
        pltpu.SMEM(tile_counts.shape, jnp.int32),
        pltpu.VMEM((rows, width), BF16),
        pltpu.VMEM((rows, width), BF16),
        pltpu.VMEM((8, Q, 2, per, rows), BF16),
        pltpu.VMEM((8, rows), F32),
        pltpu.VMEM((1, rows), F32),
        pltpu.VMEM((ITERS, 8, Q, 2, per, width), BF16),
        pltpu.VMEM((8, Q, per, width), F32),
        pltpu.VMEM((ITERS, 8, Q, per, width), BF16),
        pltpu.VMEM((ITERS, 8, Q, per, width), BF16),
        pltpu.VMEM((ITERS, 8, Q, per, width), BF16),
        pltpu.VMEM((ITERS, 3, Q, per, width), BF16),
        pltpu.VMEM((ITERS, Q, per, width), BF16),
        pltpu.VMEM((ITERS, 3, Q, per, width), BF16),
        pltpu.VMEM((Q, per, width), F32),
        pltpu.VMEM((rows, width), BF16),
        dma((N_SEMS,)), dma((N_SEMS,)), dma((16,)),
    ]
    anyspace = pl.BlockSpec(memory_space=pl.ANY)
    hbm = pl.BlockSpec(memory_space=pltpu.MemorySpace.HBM)
    shapes = (
        jax.ShapeDtypeStruct((1, mine, width), F32),
        jax.ShapeDtypeStruct((1, rows, width), BF16),
    )
    results = pl.pallas_call(
        kernel,
        out_shape=shapes,
        in_specs=[hbm, hbm, hbm],
        out_specs=(anyspace, anyspace),
        scratch_shapes=scratch,
        compiler_params=pltpu.CompilerParams(
            collective_id=0, has_side_effects=True, vmem_limit_bytes=VLIM * 1024 * 1024
        ),
    )(*[pltpu.with_memory_space_constraint(v, pltpu.MemorySpace.HBM) for v in (tile_counts, points, centroids)])
    return pl.pallas_call(
        flush,
        out_shape=shapes,
        in_specs=[anyspace, anyspace],
        out_specs=(hbm, hbm),
        scratch_shapes=[dma((5,))],
        compiler_params=pltpu.CompilerParams(vmem_limit_bytes=1024 * 1024),
    )(*results)


def solution(mesh):
    return jax.shard_map(
        body,
        mesh=mesh,
        in_specs=(P("grp", "shard", None), P("grp", "shard", None), P()),
        out_specs=(P("grp", "shard", None), P("grp", "shard", None)),
        check_vma=False,
    )
```

time: 88.4 us -> 70.1 us (0.79); the launches traced: 88.2 us -> 69 us
  Pallas kernels: 82.1 us -> 68.2 us
  local copies, waits for them, and re-layouts: 5.53 us -> 0 us
    pallas_call x1 -> x2, Pallas kernels: 82.1 us -> 68.2 us  [the longest x1 66.5 us: body(): pl.pallas_call(kernel, out_shape=shapes, in_specs=[hbm, hbm, hbm], out_sp...]
    unnamed x2 -> x0, local copies, waits for them, and re-layouts: 5.53 us -> none
where the time goes in v2:
time: 70.1 us; the launch traced here: 69 us
  Pallas kernels  68.2 us (97%)
  between operations  0.8 us (1%)
    pallas_call x1, Pallas kernels, body(): pl.pallas_call(kernel, out_shape=shapes, in_specs=[hbm, hbm, hbm], out_sp...  66.5 us
    pallas_call x1, Pallas kernels, body(): pl.pallas_call(flush, out_shape=shapes, in_specs=[anyspace, anyspace], ou...  1.79 us

profile of v2, /device:TPU:0, one launch (start us, length us, event | category | flops | bytes accessed | tf_op | source)
XLA Modules:
  0.0 69.0 jit_solution(15768188317731578801)
XLA Ops:
  0.6 66.5 %shard_map.50 = (f32[1,64,1024]{2,1,0:T(8,128)S(1)}, bf16[1,1536,1024]{2,1,0:T(8,128)(2,1)S(1)}) custom-call(s32[8]{0:T(128)} %counts_in.1, bf16[1,1536,1024]{2,1,0:T(8,128)(2,1)} %points.1, bf16[1,64,1024]{2,1,0:T(8,128)(2,1)} %cents.1), custom_call_target="tpu_custom_call" | custom-call | tf_op jit(solution)/shard_map/pallas_call | solution.py:387
  67.1 1.8 %shard_map.51 = (f32[1,64,1024]{2,1,0:T(8,128)}, bf16[1,1536,1024]{2,1,0:T(8,128)(2,1)}) custom-call(f32[1,64,1024]{2,1,0:T(8,128)S(1)} %get-tuple-element.4.newc_in, bf16[1,1536,1024]{2,1,0:T(8,128)(2,1)S(1)} %get-tuple-element.5.post_in), custom_call_target="tpu_custom_call" | custom-call | tf_op jit(solution)/shard_map/pallas_call | solution.py:397

commit v3 on v2

v3 whole, which is shorter than its diff:
```python
import math

import jax
import jax.numpy as jnp
from jax import lax
from jax.experimental import pallas as pl
from jax.experimental.pallas import tpu as pltpu
from jax.sharding import PartitionSpec as P

MESH = pl.DeviceIdType.MESH
TILE = 128
ITERS = 2
EPS = 1e-06
SHARP = 48.0
Q = 4
F32 = jnp.float32
BF16 = jnp.bfloat16
N_SEMS = 224
VLIM = 40
UNROLL = 2
YO, ZP1, ZM1, OWN, ZZ = 0, 1, 2, 3, 4


def kernel(
    counts_in, points, cents, newc, post,
    counts, pts, n, nt, e, den, inv, tab, acc, ssnd, srcv, x, r1, r2, r3, ctr, pout,
    send, recv, lsem,
):
    rows_all, width = n.shape
    per = tab.shape[4]
    g = lax.axis_index("grp")
    sh = lax.axis_index("shard")
    z, y, c = sh // 4, (sh // 2) % 2, sh % 2

    def peer(dz, dy, dc):
        zz = (z + dz) % 4
        yy = (y + dy) % 2
        cc = (c + dc) % 2
        return (g, zz * 4 + yy * 2 + cc)

    zp, zm, yo, sib = peer(1, 0, 0), peer(3, 0, 0), peer(0, 1, 0), peer(0, 0, 1)

    copies = {}
    drained = set()

    def start(key, src, dst, dev):
        i = len(copies)
        cp = pltpu.make_async_remote_copy(
            src_ref=src, dst_ref=dst, send_sem=send.at[i], recv_sem=recv.at[i],
            device_id=dev, device_id_type=MESH,
        )
        cp.start()
        copies[key] = cp

    def got(*key):
        copies[key].wait_recv()

    def drain():
        for key, cp in copies.items():
            if key not in drained:
                cp.wait_send()
                drained.add(key)

    parts = 4
    prow = rows_all // parts
    own_load = []
    for q in range(Q):
        cp = pltpu.make_async_copy(
            cents.at[0, pl.ds(q * per, per)], tab.at[0, OWN, q, 0], lsem.at[parts + q]
        )
        cp.start()
        own_load.append(cp)

    barrier = pltpu.get_barrier_semaphore()
    for dev in (zp, zm, yo, sib):
        pl.semaphore_signal(barrier, inc=1, device_id=dev, device_id_type=MESH)
    loads = []
    for i in range(parts):
        cp = pltpu.make_async_copy(
            points.at[0, pl.ds(i * prow, prow)], pts.at[pl.ds(i * prow, prow)], lsem.at[i]
        )
        cp.start()
        loads.append(cp)
    count_load = pltpu.make_async_copy(counts_in, counts, lsem.at[15])
    count_load.start()
    pl.semaphore_wait(barrier, 4)

    def hop(it, q, name, p, p_dst, dev):
        start((it, q, name), tab.at[it, p, q, 0], tab.at[it, p_dst, q, 0], dev)

    def ag_own(it, q):
        hop(it, q, "y", OWN, YO, yo)
        start((it, q, "s", OWN), tab.at[it, OWN, q, 0], tab.at[it, OWN, q, 1], sib)

    def ag_zp(it, q):
        hop(it, q, "zp", OWN, ZM1, zp)

    def ag_zm(it, q):
        hop(it, q, "zm", OWN, ZP1, zm)

    def share(it, q, p):
        start((it, q, "s", p), tab.at[it, p, q, 0], tab.at[it, p, q, 1], sib)

    def shared(it, pieces):
        for p, q in pieces:
            got(it, q, "s", p)

    def from_zp(it, q):
        got(it, q, "zp")
        if q >= 2:
            hop(it, q, "r6", ZM1, 6, yo)
        if q % 2 == 0:
            hop(it, q, "h", ZM1, ZZ, zp)
        share(it, q, ZM1)

    def from_zm(it, q):
        got(it, q, "zm")
        if q >= 2:
            hop(it, q, "r5", ZP1, 5, yo)
        if q % 2 == 1:
            hop(it, q, "h", ZP1, ZZ, zm)
        share(it, q, ZP1)

    def from_y(it, q):
        got(it, q, "y")
        if q < 2:
            hop(it, q, "r6", YO, 6, zp)
            hop(it, q, "r5", YO, 5, zm)
        share(it, q, YO)

    def from_h(it, q):
        got(it, q, "h")
        if q < 2:
            hop(it, q, "w", ZZ, 7, yo)
        share(it, q, ZZ)

    def from_side(it, q, p):
        got(it, q, "r%d" % p)
        if (q, p) == (2, 6):
            hop(it, q, "w", 6, 7, zp)
        if (q, p) == (3, 5):
            hop(it, q, "w", 5, 7, zm)
        share(it, q, p)

    def from_w(it, q):
        got(it, q, "w")
        share(it, q, 7)

    scale = SHARP / width * math.log2(math.e)
    n_rt = rows_all // 256

    def logits(it, pieces, t0=0, t1=n_rt, first=False):
        m = len(pieces) * 2 * per

        def step(rt, carry):
            at = pl.ds(pl.multiple_of(rt * 256, 256), 256)
            left = [tab[it, p, q].reshape(2 * per, width) for p, q in pieces]
            s = jnp.dot(jnp.concatenate(left, axis=0), nt[:, at], preferred_element_type=F32)
            ex = jnp.exp2(s * scale)
            part = jnp.sum(ex.reshape(m // 8, 8, 256), axis=0)
            den[:, at] = part if first else den[:, at] + part
            ex = ex.astype(BF16).reshape(len(pieces), 2, per, 256)
            for i, (p, q) in enumerate(pieces):
                e[p, q, :, :, at] = ex[i]
            return carry

        lax.fori_loop(t0, t1, step, 0, unroll=UNROLL)

    def invert():
        for t in range(rows_all // TILE):
            at = slice(t * TILE, (t + 1) * TILE)
            live = (t * 16 + sh < counts[g]).astype(F32)
            inv[:, at] = live / jnp.sum(den[:, at], axis=0, keepdims=True)

    def weigh(p0, p1, q0, q1, cores):
        nc = len(range(*cores.indices(2)))
        m = (p1 - p0) * (q1 - q0) * nc * per

        def step(j, carry):
            at = pl.ds(pl.multiple_of(j * 256, 256), 256)
            v = e[p0:p1, q0:q1, cores, :, at].reshape(m, 256).astype(F32) * inv[:, at]
            e[p0:p1, q0:q1, cores, :, at] = v.astype(BF16).reshape(p1 - p0, q1 - q0, nc, per, 256)
            return carry

        lax.fori_loop(0, n_rt, step, 0, unroll=2)

    def send_sums(it, p0, p1, q0, q1):
        for q in range(q0, q1):
            start((it, q, "x", p0), ssnd.at[it, pl.ds(p0, p1 - p0), q], srcv.at[it, pl.ds(p0, p1 - p0), q], sib)

    def sums(it, p0, p1, q0, q1, cores=slice(0, 2)):
        weigh(p0, p1, q0, q1, cores)
        nc = len(range(*cores.indices(2)))
        m = (p1 - p0) * (q1 - q0) * nc * per

        def step(ft, carry):
            at = pl.ds(pl.multiple_of(ft * 256, 256), 256)
            s = jnp.dot(
                e[p0:p1, q0:q1, cores].reshape(m, rows_all), n[:, at], preferred_element_type=F32
            ).reshape(p1 - p0, q1 - q0, nc, per, 256)
            if cores.start == 0:
                acc[p0:p1, q0:q1, :, at] = s[:, :, 0]
            if cores.stop == 2:
                ssnd[it, p0:p1, q0:q1, :, at] = s[:, :, -1].astype(BF16)
            return carry

        lax.fori_loop(0, width // 256, step, 0, unroll=2)
        if cores.stop == 2:
            send_sums(it, p0, p1, q0, q1)

    def base(it, p, q):
        return acc[p, q] + srcv[it, p, q].astype(F32)

    def give(it, q, name, i, p, value, dst, dev):
        x[it, p, q] = value.astype(BF16)
        start((it, q, name, i), x.at[it, p, q], dst, dev)

    def add1(it, q, i):
        got(it, q, "r1", i)
        return r1[it, i, q].astype(F32)

    def rs_seven(it, q):
        got(it, q, "x", 5)
        dev = yo if q < 2 else (zm if q == 2 else zp)
        give(it, q, "r1", 2, 7, base(it, 7, q), r1.at[it, 2, q], dev)

    def rs_rest(it, q):
        if q != 3:
            give(it, q, "r1", 0, 5, base(it, 5, q), r1.at[it, 0, q], zp if q < 2 else yo)
        if q != 2:
            give(it, q, "r1", 1, 6, base(it, 6, q), r1.at[it, 1, q], zm if q < 2 else yo)

    def rs_mid(it, q):
        p, i = (6, 1) if q == 2 else (5, 0)
        give(it, q, "r1", i, p, base(it, p, q) + add1(it, q, 2), r1.at[it, i, q], yo)

    def rs_two(it, q):
        got(it, q, "x", 3)
        v = base(it, ZZ, q)
        if q < 2:
            v = v + add1(it, q, 2)
        give(it, q, "r2", 0, ZZ, v, r2.at[it, q], zm if q % 2 == 0 else zp)

    def to_owner(it, q, p, v):
        slot, dev = (1, zp) if p == ZP1 else (0, zm)
        give(it, q, "r3", slot, p, v, r3.at[it, slot, q], dev)

    def rs_early(it, q):
        got(it, q, "x", 0)
        p = ZP1 if q % 2 == 0 else ZM1
        v = base(it, p, q)
        if q >= 2:
            v = v + add1(it, q, 0 if p == ZP1 else 1)
        to_owner(it, q, p, v)

    def rs_y(it, q):
        v = base(it, YO, q)
        if q < 2:
            v = v + add1(it, q, 0) + add1(it, q, 1)
        give(it, q, "r3", 2, YO, v, r3.at[it, 2, q], yo)

    def rs_three(it, q):
        got(it, q, "r2", 0)
        p = ZM1 if q % 2 == 0 else ZP1
        v = base(it, p, q) + r2[it, q].astype(F32)
        if q >= 2:
            v = v + add1(it, q, 0 if p == ZP1 else 1)
        to_owner(it, q, p, v)

    def rs_last(it, q):
        s = base(it, OWN, q)
        for i in range(3):
            got(it, q, "r3", i)
            s = s + r3[it, i, q].astype(F32)
        return s * lax.rsqrt(jnp.mean(s * s, axis=-1, keepdims=True) + EPS)

    outs = []

    def post_tile(t):
        at = slice(t * 256, (t + 1) * 256)
        w = e[:, :, :, :, at].reshape(16 * Q * per, 256)
        pout[at, :] = lax.dot_general(
            w, tab[ITERS - 1].reshape(16 * Q * per, width),
            (((0,), (0,)), ((), ())), preferred_element_type=F32,
        ).astype(BF16)
        cp = pltpu.make_async_copy(
            pout.at[pl.ds(t * 256, 256)], post.at[0, pl.ds(t * 256, 256)], lsem.at[parts + Q + t]
        )
        cp.start()
        outs.append(cp)

    for cp in own_load:
        cp.wait()
    for i in range(Q):
        ag_zp(0, (0, 2, 3, 1)[i])
        ag_zm(0, (1, 3, 2, 0)[i])
        ag_own(0, i)

    def unit(j, carry):
        at = pl.ds(pl.multiple_of(j * 32, 32), 32)
        v = pts[at, :].astype(F32)
        n[at, :] = (v * lax.rsqrt(jnp.mean(v * v, axis=-1, keepdims=True) + EPS)).astype(BF16)
        return carry

    for i in range(parts):
        loads[i].wait()
        lax.fori_loop(i * prow // 32, (i + 1) * prow // 32, unit, 0, unroll=2)
    count_load.wait()

    def turn(j, carry):
        at = pl.ds(pl.multiple_of(j * 128, 128), 128)
        nt[:, at] = n[at, :].T
        return carry

    lax.fori_loop(0, rows_all // 256, turn, 0)

    for it in range(ITERS):
        last = it == ITERS - 1
        if it > 0:
            drain()
        from_zp(it, 0)
        from_zm(it, 1)
        from_y(it, 0)
        if it == 0:
            lax.fori_loop(rows_all // 256, rows_all // 128, turn, 0)
        from_zp(it, 2)
        from_zm(it, 3)
        from_y(it, 1)
        from_zp(it, 3)
        from_zm(it, 2)
        from_y(it, 2)
        now = [(YO, 0), (YO, 1), (ZM1, 0), (ZM1, 2), (ZP1, 1), (ZP1, 3)]
        shared(it, now)
        logits(it, now, 0, 2, first=True)
        from_zp(it, 1)
        from_zm(it, 0)
        from_y(it, 3)
        logits(it, now, 2, 6, first=True)
        from_h(it, 0)
        from_h(it, 1)
        now = [(YO, 2), (YO, 3), (ZM1, 3), (ZM1, 1), (ZP1, 2), (ZP1, 0)]
        shared(it, now)
        logits(it, now, 0, 2)
        from_side(it, 2, 6)
        from_side(it, 0, 5)
        from_side(it, 0, 6)
        logits(it, now, 2, 6)
        from_side(it, 3, 5)
        from_h(it, 2)
        from_h(it, 3)
        now = [(OWN, 0), (OWN, 1), (OWN, 2), (OWN, 3), (ZZ, 0), (ZZ, 1)]
        shared(it, now)
        logits(it, now, 0, 4)
        from_side(it, 1, 5)
        from_side(it, 1, 6)
        from_side(it, 3, 6)
        logits(it, now, 4, 6)
        now = [(ZZ, 2), (ZZ, 3), (5, 0), (6, 0), (6, 2), (5, 3)]
        shared(it, now)
        logits(it, now, 0, 2)
        from_side(it, 2, 5)
        logits(it, now, 2, 6)
        from_w(it, 0)
        from_w(it, 2)
        now = [(5, 1), (6, 1), (6, 3), (5, 2)]
        shared(it, now)
        logits(it, now, 0, 4)
        from_w(it, 1)
        from_w(it, 3)
        logits(it, now, 4, 6)
        now = [(7, 0), (7, 1), (7, 2), (7, 3)]
        shared(it, now)
        logits(it, now)
        invert()

        def fill(t):
            if last:
                post_tile(t)

        sums(it, 5, 8, 0, 4, slice(1, 2))
        sums(it, 5, 8, 0, 4, slice(0, 1))
        for q in range(Q):
            rs_seven(it, q)
        for q in range(Q):
            rs_rest(it, q)
        sums(it, 3, 5, 0, 4)
        sums(it, 0, 3, 0, 2)
        rs_two(it, 2)
        rs_two(it, 3)
        rs_two(it, 0)
        rs_mid(it, 2)
        sums(it, 0, 3, 2, 4)
        rs_two(it, 1)
        rs_mid(it, 3)
        rs_early(it, 0)
        rs_early(it, 1)
        rs_y(it, 0)
        rs_y(it, 1)
        fill(0)
        rs_early(it, 2)
        rs_early(it, 3)
        rs_y(it, 2)
        rs_y(it, 3)
        rs_three(it, 0)
        fill(1)
        rs_three(it, 1)
        rs_three(it, 2)
        fill(2)
        rs_three(it, 3)
        fill(3)
        if last:
            drain()
        fill(4)
        fill(5)
        for q in range(Q):
            s = rs_last(it, q)
            if last:
                ctr[q] = s
                cp = pltpu.make_async_copy(
                    ctr.at[q], newc.at[0, pl.ds(q * per, per)], lsem.at[parts + q]
                )
                cp.start()
                outs.append(cp)
            else:
                tab[it + 1, OWN, q, 0] = s.astype(BF16)
                ag_zp(it + 1, q)
                ag_zm(it + 1, q)
                ag_own(it + 1, q)
    drain()
    for cp in outs:
        cp.wait()


def flush(newc_in, post_in, newc, post, sems):
    rows = post.shape[1]
    parts = 4
    cut = rows // parts
    cps = [pltpu.make_async_copy(newc_in, newc, sems.at[parts])]
    for i in range(parts):
        at = pl.ds(i * cut, cut)
        cps.append(pltpu.make_async_copy(post_in.at[0, at], post.at[0, at], sems.at[i]))
    for cp in cps:
        cp.start()
    for cp in cps:
        cp.wait()


def body(points, centroids, tile_counts):
    rows, width = points.shape[1:]
    mine = centroids.shape[1]
    per = mine // Q
    dma = pltpu.SemaphoreType.DMA
    scratch = [
        pltpu.SMEM(tile_counts.shape, jnp.int32),
        pltpu.VMEM((rows, width), BF16),
        pltpu.VMEM((rows, width), BF16),
        pltpu.VMEM((width, rows), BF16),
        pltpu.VMEM((8, Q, 2, per, rows), BF16),
        pltpu.VMEM((8, rows), F32),
        pltpu.VMEM((1, rows), F32),
        pltpu.VMEM((ITERS, 8, Q, 2, per, width), BF16),
        pltpu.VMEM((8, Q, per, width), F32),
        pltpu.VMEM((ITERS, 8, Q, per, width), BF16),
        pltpu.VMEM((ITERS, 8, Q, per, width), BF16),
        pltpu.VMEM((ITERS, 8, Q, per, width), BF16),
        pltpu.VMEM((ITERS, 3, Q, per, width), BF16),
        pltpu.VMEM((ITERS, Q, per, width), BF16),
        pltpu.VMEM((ITERS, 3, Q, per, width), BF16),
        pltpu.VMEM((Q, per, width), F32),
        pltpu.VMEM((rows, width), BF16),
        dma((N_SEMS,)), dma((N_SEMS,)), dma((16,)),
    ]
    anyspace = pl.BlockSpec(memory_space=pl.ANY)
    hbm = pl.BlockSpec(memory_space=pltpu.MemorySpace.HBM)
    shapes = (
        jax.ShapeDtypeStruct((1, mine, width), F32),
        jax.ShapeDtypeStruct((1, rows, width), BF16),
    )
    results = pl.pallas_call(
        kernel,
        out_shape=shapes,
        in_specs=[hbm, hbm, hbm],
        out_specs=(anyspace, anyspace),
        scratch_shapes=scratch,
        compiler_params=pltpu.CompilerParams(
            collective_id=0, has_side_effects=True, vmem_limit_bytes=VLIM * 1024 * 1024
        ),
    )(*[pltpu.with_memory_space_constraint(v, pltpu.MemorySpace.HBM) for v in (tile_counts, points, centroids)])
    return pl.pallas_call(
        flush,
        out_shape=shapes,
        in_specs=[anyspace, anyspace],
        out_specs=(hbm, hbm),
        scratch_shapes=[dma((5,))],
        compiler_params=pltpu.CompilerParams(vmem_limit_bytes=1024 * 1024),
    )(*results)


def solution(mesh):
    return jax.shard_map(
        body,
        mesh=mesh,
        in_specs=(P("grp", "shard", None), P("grp", "shard", None), P()),
        out_specs=(P("grp", "shard", None), P("grp", "shard", None)),
        check_vma=False,
    )
```

time: 70.1 us -> 68.7 us (0.980); the launches traced: 69 us -> 68.6 us
  no operation moved by 1% of the time
where the time goes in v3:
time: 68.7 us; the launch traced here: 68.6 us
  Pallas kernels  67.8 us (99%)
  between operations  0.8 us (1%)
    pallas_call x1, Pallas kernels, body(): pl.pallas_call(kernel, out_shape=shapes, in_specs=[hbm, hbm, hbm], out_sp...  66 us
    pallas_call x1, Pallas kernels, body(): pl.pallas_call(flush, out_shape=shapes, in_specs=[anyspace, anyspace], ou...  1.79 us

profile of v3, /device:TPU:0, one launch (start us, length us, event | category | flops | bytes accessed | tf_op | source)
XLA Modules:
  0.0 68.6 jit_solution(9537481451576020680)
XLA Ops:
  0.6 66.0 %shard_map.50 = (f32[1,64,1024]{2,1,0:T(8,128)S(1)}, bf16[1,1536,1024]{2,1,0:T(8,128)(2,1)S(1)}) custom-call(s32[8]{0:T(128)} %counts_in.1, bf16[1,1536,1024]{2,1,0:T(8,128)(2,1)} %points.1, bf16[1,64,1024]{2,1,0:T(8,128)(2,1)} %cents.1), custom_call_target="tpu_custom_call" | custom-call | tf_op jit(solution)/shard_map/pallas_call | solution.py:479
  66.6 1.8 %shard_map.51 = (f32[1,64,1024]{2,1,0:T(8,128)}, bf16[1,1536,1024]{2,1,0:T(8,128)(2,1)}) custom-call(f32[1,64,1024]{2,1,0:T(8,128)S(1)} %get-tuple-element.4.newc_in, bf16[1,1536,1024]{2,1,0:T(8,128)(2,1)S(1)} %get-tuple-element.5.post_in), custom_call_target="tpu_custom_call" | custom-call | tf_op jit(solution)/shard_map/pallas_call | solution.py:489

commit v4 on v3

--- a/solution.py
+++ b/solution.py
@@ -172,41 +172,37 @@
             live = (t * 16 + sh < counts[g]).astype(F32)
             inv[:, at] = live / jnp.sum(den[:, at], axis=0, keepdims=True)
 
-    def weigh(p0, p1, q0, q1, cores):
-        nc = len(range(*cores.indices(2)))
-        m = (p1 - p0) * (q1 - q0) * nc * per
+    def weigh(p0, p1, q0, q1):
+        m = (p1 - p0) * (q1 - q0) * 2 * per
 
         def step(j, carry):
             at = pl.ds(pl.multiple_of(j * 256, 256), 256)
-            v = e[p0:p1, q0:q1, cores, :, at].reshape(m, 256).astype(F32) * inv[:, at]
-            e[p0:p1, q0:q1, cores, :, at] = v.astype(BF16).reshape(p1 - p0, q1 - q0, nc, per, 256)
+            v = e[p0:p1, q0:q1, :, :, at].reshape(m, 256).astype(F32) * inv[:, at]
+            e[p0:p1, q0:q1, :, :, at] = v.astype(BF16).reshape(p1 - p0, q1 - q0, 2, per, 256)
             return carry
 
         lax.fori_loop(0, n_rt, step, 0, unroll=2)
 
-    def send_sums(it, p0, p1, q0, q1):
-        for q in range(q0, q1):
-            start((it, q, "x", p0), ssnd.at[it, pl.ds(p0, p1 - p0), q], srcv.at[it, pl.ds(p0, p1 - p0), q], sib)
-
-    def sums(it, p0, p1, q0, q1, cores=slice(0, 2)):
-        weigh(p0, p1, q0, q1, cores)
-        nc = len(range(*cores.indices(2)))
-        m = (p1 - p0) * (q1 - q0) * nc * per
+    n_ft = width // 256
+
+    def sums(it, p0, p1, q0, q1, f0=0, f1=n_ft):
+        m = (p1 - p0) * (q1 - q0) * 2 * per
+        if f0 == 0:
+            weigh(p0, p1, q0, q1)
 
         def step(ft, carry):
             at = pl.ds(pl.multiple_of(ft * 256, 256), 256)
             s = jnp.dot(
-                e[p0:p1, q0:q1, cores].reshape(m, rows_all), n[:, at], preferred_element_type=F32
-            ).reshape(p1 - p0, q1 - q0, nc, per, 256)
-            if cores.start == 0:
-                acc[p0:p1, q0:q1, :, at] = s[:, :, 0]
-            if cores.stop == 2:
-                ssnd[it, p0:p1, q0:q1, :, at] = s[:, :, -1].astype(BF16)
+                e[p0:p1, q0:q1].reshape(m, rows_all), n[:, at], preferred_element_type=F32
+            ).reshape(p1 - p0, q1 - q0, 2, per, 256)
+            acc[p0:p1, q0:q1, :, at] = s[:, :, 0]
+            ssnd[it, p0:p1, q0:q1, :, at] = s[:, :, 1].astype(BF16)
             return carry
 
-        lax.fori_loop(0, width // 256, step, 0, unroll=2)
-        if cores.stop == 2:
-            send_sums(it, p0, p1, q0, q1)
+        lax.fori_loop(f0, f1, step, 0, unroll=2)
+        if f1 == n_ft:
+            for q in range(q0, q1):
+                start((it, q, "x", p0), ssnd.at[it, pl.ds(p0, p1 - p0), q], srcv.at[it, pl.ds(p0, p1 - p0), q], sib)
 
     def base(it, p, q):
         return acc[p, q] + srcv[it, p, q].astype(F32)
@@ -220,11 +216,12 @@
         return r1[it, i, q].astype(F32)
 
     def rs_seven(it, q):
-        got(it, q, "x", 5)
+        got(it, q, "x", 7)
         dev = yo if q < 2 else (zm if q == 2 else zp)
         give(it, q, "r1", 2, 7, base(it, 7, q), r1.at[it, 2, q], dev)
 
     def rs_rest(it, q):
+        got(it, q, "x", 5)
         if q != 3:
             give(it, q, "r1", 0, 5, base(it, 5, q), r1.at[it, 0, q], zp if q < 2 else yo)
         if q != 2:
@@ -377,35 +374,36 @@
             if last:
                 post_tile(t)
 
-        sums(it, 5, 8, 0, 4, slice(1, 2))
-        sums(it, 5, 8, 0, 4, slice(0, 1))
-        for q in range(Q):
+        sums(it, 7, 8, 0, 4)
+        sums(it, 5, 7, 0, 4)
+        for q in (2, 3, 0, 1):
             rs_seven(it, q)
+        sums(it, 3, 5, 0, 4)
         for q in range(Q):
             rs_rest(it, q)
-        sums(it, 3, 5, 0, 4)
         sums(it, 0, 3, 0, 2)
         rs_two(it, 2)
         rs_two(it, 3)
+        sums(it, 0, 3, 2, 4, 0, 2)
         rs_two(it, 0)
         rs_mid(it, 2)
-        sums(it, 0, 3, 2, 4)
+        sums(it, 0, 3, 2, 4, 2, 4)
         rs_two(it, 1)
         rs_mid(it, 3)
         rs_early(it, 0)
         rs_early(it, 1)
+        fill(0)
         rs_y(it, 0)
         rs_y(it, 1)
-        fill(0)
         rs_early(it, 2)
         rs_early(it, 3)
         rs_y(it, 2)
         rs_y(it, 3)
+        fill(1)
         rs_three(it, 0)
-        fill(1)
-        rs_three(it, 1)
         rs_three(it, 2)
         fill(2)
+        rs_three(it, 1)
         rs_three(it, 3)
         fill(3)
         if last:

time: 68.7 us -> 67.3 us (0.980)
  Pallas kernels: 67.8 us -> 66.4 us
    pallas_call x1, Pallas kernels: 66 us -> 64.6 us  [body(): pl.pallas_call(kernel, out_shape=shapes, in_specs=[hbm, hbm, hbm], out_sp...]
where the time goes in v4:
time: 67.3 us; the launch traced here: 67.2 us
  Pallas kernels  66.4 us (99%)
  between operations  0.8 us (1%)
    pallas_call x1, Pallas kernels, body(): pl.pallas_call(kernel, out_shape=shapes, in_specs=[hbm, hbm, hbm], out_sp...  64.6 us
    pallas_call x1, Pallas kernels, body(): pl.pallas_call(flush, out_shape=shapes, in_specs=[anyspace, anyspace], ou...  1.79 us

profile of v4, /device:TPU:0, one launch (start us, length us, event | category | flops | bytes accessed | tf_op | source)
XLA Modules:
  0.0 67.2 jit_solution(16015058890165431922)
XLA Ops:
  0.6 64.6 %shard_map.50 = (f32[1,64,1024]{2,1,0:T(8,128)S(1)}, bf16[1,1536,1024]{2,1,0:T(8,128)(2,1)S(1)}) custom-call(s32[8]{0:T(128)} %counts_in.1, bf16[1,1536,1024]{2,1,0:T(8,128)(2,1)} %points.1, bf16[1,64,1024]{2,1,0:T(8,128)(2,1)} %cents.1), custom_call_target="tpu_custom_call" | custom-call | tf_op jit(solution)/shard_map/pallas_call | solution.py:477
  65.3 1.8 %shard_map.51 = (f32[1,64,1024]{2,1,0:T(8,128)}, bf16[1,1536,1024]{2,1,0:T(8,128)(2,1)}) custom-call(f32[1,64,1024]{2,1,0:T(8,128)S(1)} %get-tuple-element.4.newc_in, bf16[1,1536,1024]{2,1,0:T(8,128)(2,1)S(1)} %get-tuple-element.5.post_in), custom_call_target="tpu_custom_call" | custom-call | tf_op jit(solution)/shard_map/pallas_call | solution.py:487

commit v5 on v4

--- a/solution.py
+++ b/solution.py
@@ -177,7 +177,7 @@
 
         def step(j, carry):
             at = pl.ds(pl.multiple_of(j * 256, 256), 256)
-            v = e[p0:p1, q0:q1, :, :, at].reshape(m, 256).astype(F32) * inv[:, at]
+            v = e[p0:p1, q0:q1, :, :, at].reshape(m, 256) * inv[:, at].astype(BF16)
             e[p0:p1, q0:q1, :, :, at] = v.astype(BF16).reshape(p1 - p0, q1 - q0, 2, per, 256)
             return carry
 
@@ -410,7 +410,7 @@
             drain()
         fill(4)
         fill(5)
-        for q in range(Q):
+        for q in (0, 2, 1, 3):
             s = rs_last(it, q)
             if last:
                 ctr[q] = s

time: 67.3 us -> 66.3 us (0.985)
  Pallas kernels: 66.4 us -> 65.4 us
    pallas_call x1, Pallas kernels: 64.6 us -> 63.6 us  [body(): pl.pallas_call(kernel, out_shape=shapes, in_specs=[hbm, hbm, hbm], out_sp...]
where the time goes in v5:
time: 66.3 us; the launch traced here: 66.2 us
  Pallas kernels  65.4 us (99%)
  between operations  0.8 us (1%)
    pallas_call x1, Pallas kernels, body(): pl.pallas_call(kernel, out_shape=shapes, in_specs=[hbm, hbm, hbm], out_sp...  63.6 us
    pallas_call x1, Pallas kernels, body(): pl.pallas_call(flush, out_shape=shapes, in_specs=[anyspace, anyspace], ou...  1.79 us

profile of v5, /device:TPU:0, one launch (start us, length us, event | category | flops | bytes accessed | tf_op | source)
XLA Modules:
  0.0 66.2 jit_solution(17451526953606788562)
XLA Ops:
  0.6 63.6 %shard_map.50 = (f32[1,64,1024]{2,1,0:T(8,128)S(1)}, bf16[1,1536,1024]{2,1,0:T(8,128)(2,1)S(1)}) custom-call(s32[8]{0:T(128)} %counts_in.1, bf16[1,1536,1024]{2,1,0:T(8,128)(2,1)} %points.1, bf16[1,64,1024]{2,1,0:T(8,128)(2,1)} %cents.1), custom_call_target="tpu_custom_call" | custom-call | tf_op jit(solution)/shard_map/pallas_call | solution.py:477
  64.2 1.8 %shard_map.51 = (f32[1,64,1024]{2,1,0:T(8,128)}, bf16[1,1536,1024]{2,1,0:T(8,128)(2,1)}) custom-call(f32[1,64,1024]{2,1,0:T(8,128)S(1)} %get-tuple-element.4.newc_in, bf16[1,1536,1024]{2,1,0:T(8,128)(2,1)S(1)} %get-tuple-element.5.post_in), custom_call_target="tpu_custom_call" | custom-call | tf_op jit(solution)/shard_map/pallas_call | solution.py:487

commit v6 on v5

--- a/solution.py
+++ b/solution.py
@@ -23,7 +23,7 @@
 
 def kernel(
     counts_in, points, cents, newc, post,
-    counts, pts, n, nt, e, den, inv, tab, acc, ssnd, srcv, x, r1, r2, r3, ctr, pout,
+    counts, pts, n, nt, e, den, inv, tab, acc, ssnd, srcv, x, r1, r2, r3,
     send, recv, lsem,
 ):
     rows_all, width = n.shape
@@ -271,20 +271,14 @@
             s = s + r3[it, i, q].astype(F32)
         return s * lax.rsqrt(jnp.mean(s * s, axis=-1, keepdims=True) + EPS)
 
-    outs = []
 
     def post_tile(t):
         at = slice(t * 256, (t + 1) * 256)
         w = e[:, :, :, :, at].reshape(16 * Q * per, 256)
-        pout[at, :] = lax.dot_general(
+        post[0, at, :] = lax.dot_general(
             w, tab[ITERS - 1].reshape(16 * Q * per, width),
             (((0,), (0,)), ((), ())), preferred_element_type=F32,
         ).astype(BF16)
-        cp = pltpu.make_async_copy(
-            pout.at[pl.ds(t * 256, 256)], post.at[0, pl.ds(t * 256, 256)], lsem.at[parts + Q + t]
-        )
-        cp.start()
-        outs.append(cp)
 
     for cp in own_load:
         cp.wait()
@@ -309,7 +303,6 @@
         nt[:, at] = n[at, :].T
         return carry
 
-    lax.fori_loop(0, rows_all // 256, turn, 0)
 
     for it in range(ITERS):
         last = it == ITERS - 1
@@ -319,10 +312,12 @@
         from_zm(it, 1)
         from_y(it, 0)
         if it == 0:
-            lax.fori_loop(rows_all // 256, rows_all // 128, turn, 0)
+            lax.fori_loop(0, rows_all // 256, turn, 0)
         from_zp(it, 2)
         from_zm(it, 3)
         from_y(it, 1)
+        if it == 0:
+            lax.fori_loop(rows_all // 256, rows_all // 128, turn, 0)
         from_zp(it, 3)
         from_zm(it, 2)
         from_y(it, 2)
@@ -413,20 +408,13 @@
         for q in (0, 2, 1, 3):
             s = rs_last(it, q)
             if last:
-                ctr[q] = s
-                cp = pltpu.make_async_copy(
-                    ctr.at[q], newc.at[0, pl.ds(q * per, per)], lsem.at[parts + q]
-                )
-                cp.start()
-                outs.append(cp)
+                newc[0, q * per:(q + 1) * per] = s
             else:
                 tab[it + 1, OWN, q, 0] = s.astype(BF16)
                 ag_zp(it + 1, q)
                 ag_zm(it + 1, q)
                 ag_own(it + 1, q)
     drain()
-    for cp in outs:
-        cp.wait()
 
 
 def flush(newc_in, post_in, newc, post, sems):
@@ -464,8 +452,6 @@
         pltpu.VMEM((ITERS, 3, Q, per, width), BF16),
         pltpu.VMEM((ITERS, Q, per, width), BF16),
         pltpu.VMEM((ITERS, 3, Q, per, width), BF16),
-        pltpu.VMEM((Q, per, width), F32),
-        pltpu.VMEM((rows, width), BF16),
         dma((N_SEMS,)), dma((N_SEMS,)), dma((16,)),
     ]
     anyspace = pl.BlockSpec(memory_space=pl.ANY)
@@ -478,7 +464,7 @@
         kernel,
         out_shape=shapes,
         in_specs=[hbm, hbm, hbm],
-        out_specs=(anyspace, anyspace),
+        out_specs=(pl.BlockSpec(memory_space=pltpu.MemorySpace.VMEM),) * 2,
         scratch_shapes=scratch,
         compiler_params=pltpu.CompilerParams(
             collective_id=0, has_side_effects=True, vmem_limit_bytes=VLIM * 1024 * 1024

time: 66.3 us -> 66 us (level)
  no operation moved by 1% of the time
where the time goes in v6:
time: 66 us; the launch traced here: 65.9 us
  Pallas kernels  65.1 us (99%)
  between operations  0.8 us (1%)
    pallas_call x1, Pallas kernels, body(): pl.pallas_call(kernel, out_shape=shapes, in_specs=[hbm, hbm, hbm], out_sp...  63.3 us
    pallas_call x1, Pallas kernels, body(): pl.pallas_call(flush, out_shape=shapes, in_specs=[anyspace, anyspace], ou...  1.79 us

profile of v6, /device:TPU:0, one launch (start us, length us, event | category | flops | bytes accessed | tf_op | source)
XLA Modules:
  0.0 65.9 jit_solution(3146218403348075738)
XLA Ops:
  0.6 63.3 %shard_map.50 = (f32[1,64,1024]{2,1,0:T(8,128)S(1)}, bf16[1,1536,1024]{2,1,0:T(8,128)(2,1)S(1)}) custom-call(s32[8]{0:T(128)} %counts_in.1, bf16[1,1536,1024]{2,1,0:T(8,128)(2,1)} %points.1, bf16[1,64,1024]{2,1,0:T(8,128)(2,1)} %cents.1), custom_call_target="tpu_custom_call" | custom-call | tf_op jit(solution)/shard_map/pallas_call | solution.py:463
  63.9 1.8 %shard_map.51 = (f32[1,64,1024]{2,1,0:T(8,128)}, bf16[1,1536,1024]{2,1,0:T(8,128)(2,1)}) custom-call(f32[1,64,1024]{2,1,0:T(8,128)S(1)} %get-tuple-element.4.newc_in, bf16[1,1536,1024]{2,1,0:T(8,128)(2,1)S(1)} %get-tuple-element.5.post_in), custom_call_target="tpu_custom_call" | custom-call | tf_op jit(solution)/shard_map/pallas_call | solution.py:473

commit v7 on v6

--- a/solution.py
+++ b/solution.py
@@ -387,8 +387,8 @@
         rs_mid(it, 3)
         rs_early(it, 0)
         rs_early(it, 1)
+        rs_y(it, 0)
         fill(0)
-        rs_y(it, 0)
         rs_y(it, 1)
         rs_early(it, 2)
         rs_early(it, 3)

time: 66 us -> 66 us (level)
  no operation moved by 1% of the time
where the time goes in v7:
time: 66 us; the launch traced here: 65.9 us
  Pallas kernels  65.1 us (99%)
  between operations  0.8 us (1%)
    pallas_call x1, Pallas kernels, body(): pl.pallas_call(kernel, out_shape=shapes, in_specs=[hbm, hbm, hbm], out_sp...  63.3 us
    pallas_call x1, Pallas kernels, body(): pl.pallas_call(flush, out_shape=shapes, in_specs=[anyspace, anyspace], ou...  1.79 us

profile of v7, /device:TPU:0, one launch (start us, length us, event | category | flops | bytes accessed | tf_op | source)
XLA Modules:
  0.0 65.9 jit_solution(10594873130102353648)
XLA Ops:
  0.6 63.3 %shard_map.50 = (f32[1,64,1024]{2,1,0:T(8,128)S(1)}, bf16[1,1536,1024]{2,1,0:T(8,128)(2,1)S(1)}) custom-call(s32[8]{0:T(128)} %counts_in.1, bf16[1,1536,1024]{2,1,0:T(8,128)(2,1)} %points.1, bf16[1,64,1024]{2,1,0:T(8,128)(2,1)} %cents.1), custom_call_target="tpu_custom_call" | custom-call | tf_op jit(solution)/shard_map/pallas_call | solution.py:463
  63.9 1.8 %shard_map.51 = (f32[1,64,1024]{2,1,0:T(8,128)}, bf16[1,1536,1024]{2,1,0:T(8,128)(2,1)}) custom-call(f32[1,64,1024]{2,1,0:T(8,128)S(1)} %get-tuple-element.4.newc_in, bf16[1,1536,1024]{2,1,0:T(8,128)(2,1)S(1)} %get-tuple-element.5.post_in), custom_call_target="tpu_custom_call" | custom-call | tf_op jit(solution)/shard_map/pallas_call | solution.py:473
